TPU v7x, 32 devices: a whole 2x2x4 slice. The times are simulated.
32 devices in a mesh: section: 4 (over z), space: 8 (over y, x, core).
Axes of the slice: x: 2, y: 2, z: 4, core: 2. Of those that a mesh axis runs over, the one named last changes fastest.
Arguments:
- features: bfloat16 [1, 32, 128, 320], P(None, 'space'), may hold values from -30 to 30
- section_packs: bfloat16 [4, 11520, 640], P('section', None, 'space'), may hold values from -6 to 6
Outputs:
- output: bfloat16 [1, 32, 128, 320], P(None, 'space', 'section')
All inputs are finite; a program needn't handle non-finite values.
Results may differ from a plain program's by a relative error of at most 0.009.
Values may be sent and summed in bfloat16 or wider, within the bound.
No kernel may reach another device: no remote copies, remote signals or barrier semaphores. Data moves between devices by JAX's collectives and lax.ppermute only.
A program may use at most 128 MiB of HBM per device.

v0:
```python
from functools import partial
import math

import jax
import jax.numpy as jnp
from jax import lax
from jax.experimental import pallas as pl
from jax.experimental.pallas import tpu as pltpu
from jax.sharding import PartitionSpec as P

GROUPS = 32
EPSILON = 1e-05
TAIL = 16
BF16 = jnp.bfloat16
F32 = jnp.float32


def row_stack(rows, count, width):
    ids = lax.broadcasted_iota(jnp.int32, (count, width), 0)
    total = jnp.zeros((count, width), F32)
    for place, row in enumerate(rows):
        total = jnp.where(ids == place, row, total)
    return total


def bf16_terms(row):
    high = row.astype(BF16).astype(F32)
    rest = row - high
    mid = rest.astype(BF16).astype(F32)
    return [high, mid, (rest - mid).astype(BF16).astype(F32)]


def moments_of(value):
    return [
        jnp.sum(value, axis=0, keepdims=True),
        jnp.sum(value * value, axis=0, keepdims=True),
    ]


def group_terms(sums, count):
    width = sums.shape[1]
    size = width // GROUPS
    terms = row_stack(bf16_terms(sums[0:1]) + bf16_terms(sums[1:2]), 16, width).astype(BF16)
    left = lax.broadcasted_iota(jnp.int32, (width, width), 0) // size
    right = lax.broadcasted_iota(jnp.int32, (width, width), 1) // size
    together = jnp.where(left == right, 1.0, 0.0).astype(BF16)
    summed = jnp.dot(terms, together, preferred_element_type=F32) * (1.0 / (count * size))
    mean = summed[0:1] + summed[1:2] + summed[2:3]
    square = summed[3:4] + summed[4:5] + summed[5:6]
    variance = jnp.maximum(square - mean * mean, 0.0)
    return mean, lax.rsqrt(variance + EPSILON)


def silu(z):
    half = 0.5 * z
    return half + half * jnp.tanh(half)


def parity_matrix(width):
    source = lax.broadcasted_iota(jnp.int32, (width, width), 0)
    target = lax.broadcasted_iota(jnp.int32, (width, width), 1)
    half = width // 2
    wanted = jnp.where(target < half, 2 * target, 2 * (target - half) + 1)
    return jnp.where(source == wanted, 1.0, 0.0).astype(BF16)


def shifted(value, step):
    rows = value.shape[0]
    ids = lax.broadcasted_iota(jnp.int32, value.shape, 0)
    if step == 1:
        return jnp.where(ids == 0, 0.0, pltpu.roll(value, 1, 0))
    return jnp.where(ids == rows - 1, 0.0, pltpu.roll(value, rows - 1, 0))


class Shape:
    def __init__(self, features, packs, n):
        self.n = n
        self.rows = features.shape[1]
        self.cols = features.shape[2]
        self.half = self.cols // 2
        self.narrow = features.shape[3]
        self.wide = 2 * self.narrow
        self.m = min(n, 8)
        self.cols_of = self.wide // self.m
        self.blk = 3 * self.narrow // 2
        self.lanes = -(-self.blk // 128) * 128
        self.fine_count = self.rows * n * self.cols
        self.coarse_count = self.fine_count // 4


def emit(flags, out_ref, outer_ref, inner_ref, stats_ref, keep, rows, width, sums):
    channels = out_ref.shape[1]
    core0 = flags[0] == 0
    tail = row_stack(bf16_terms(sums[0]) + bf16_terms(sums[1]), TAIL, channels).astype(BF16)
    out_ref[rows * width :, :] = tail
    stats_ref[...] = row_stack(sums, 8, channels)
    size = keep * width
    first = out_ref[0:size, :].astype(F32)
    last = out_ref[(rows - keep) * width : rows * width, :].astype(F32)
    outer_ref[0:size, :] = jnp.where(core0, first, last).astype(BF16)
    outer_ref[size:, :] = tail
    inner_ref[...] = jnp.where(core0, last, first).astype(BF16)


def ext_row(index, block_ref, outer_ref, inner_ref, flags, rows, halo, width):
    if index < halo:
        span = slice(index * width, (index + 1) * width)
        pick = jnp.where(flags[0] == 0, outer_ref[span, :].astype(F32), inner_ref[span, :].astype(F32))
        return pick, flags[1] != 0
    index -= halo
    if index < rows:
        return block_ref[index * width : (index + 1) * width, :].astype(F32), None
    index -= rows
    span = slice(index * width, (index + 1) * width)
    pick = jnp.where(flags[0] == 0, inner_ref[span, :].astype(F32), outer_ref[span, :].astype(F32))
    return pick, flags[2] != 0


def masked(value, outside):
    if outside is None:
        return value
    return jnp.where(outside, 0.0, value)


class Weights:
    def __init__(self, shape, bounds, start, c_in, c_out):
        self.shape = shape
        self.c_in = c_in
        self.c_out = c_out
        self.split = c_out != shape.wide
        self.blocks = 3 * c_in * c_out // shape.wide // shape.blk
        self.start = start // shape.blk
        self.bounds = bounds
        self.depth = self.blocks * shape.lanes
        self.width = (2 if self.split else 1) * self.depth

    def stacks(self, refs):
        refs = list(refs)
        return {low: [refs.pop(0) for _ in owners] for low, _, owners in self.bounds}

    def copies(self, flags, stack_refs, buffer, sems):
        made = []
        for dy in range(3):
            mine = []
            for block in range(self.blocks):
                at = self.start + dy * self.blocks + block
                for low, high, owners in self.bounds:
                    if low <= at < high:
                        for ref, owner in zip(stack_refs[low], owners, strict=True):
                            for j in range(ref.shape[0]):
                                mine.append(
                                    pltpu.make_async_copy(
                                        ref.at[j, at - low],
                                        buffer.at[dy, block, owner(flags, j)],
                                        sems.at[dy, len(mine)],
                                    )
                                )
            made.append(mine)
        return made

    def product(self, left, buffer, dy):
        shape = self.shape
        rows = shape.m * shape.cols_of
        total = None
        for block in range(self.blocks):
            right = buffer[dy, block].reshape(rows, shape.lanes)
            for odd in range(2 if self.split else 1):
                part = right[odd * self.c_out : (odd + 1) * self.c_out] if self.split else right
                begin = (odd * self.blocks + block) * shape.lanes
                made = lax.dot_general(
                    left[:, begin : begin + shape.lanes], part, (((1,), (1,)), ((), ())), preferred_element_type=F32
                )
                total = made if total is None else total + made
        return total

    def put(self, image, row, place, tap, value, first=0, channels=None):
        shape = self.shape
        size = value.shape[0]
        half = self.c_in // 2
        runs = []
        if self.split:
            c = value.shape[1] // 2
            runs = [(odd, tap * half + first // 2, odd * c, c) for odd in range(2)]
        else:
            runs = [(0, tap * self.c_in + first, 0, value.shape[1])]
        for odd, index, at, left in runs:
            while left > 0:
                step = min(left, shape.blk - index % shape.blk)
                lane = odd * self.depth + index // shape.blk * shape.lanes + index % shape.blk
                image[row, place : place + size, lane : lane + step] = value[:, at : at + step]
                index, at, left = index + step, at + step, left - step

    def clear(self, image):
        shape = self.shape
        for block in range(self.width // shape.lanes):
            begin = block * shape.lanes + shape.blk
            end = (block + 1) * shape.lanes
            image[:, :, begin:end] = jnp.zeros((image.shape[0], image.shape[1], end - begin), BF16)


def fine_columns(store, row, width, even, odd):
    half = even.shape[0]
    store(row, 0, half, 0, shifted(odd, 1))
    store(row, 0, half, 1, even)
    store(row, 0, half, 2, odd)
    store(row, half, half, 0, even)
    store(row, half, half, 1, odd)
    store(row, half, half, 2, shifted(even, -1))


def run_conv(weights, buffer, image, acc, copies, rows, width):
    for dy in range(3):
        for copy in copies[dy]:
            copy.wait()
        left = image[dy : dy + rows].reshape(rows * width, weights.width)
        made = weights.product(left, buffer, dy)
        if dy == 0:
            acc[...] = made
        else:
            acc[...] += made


def scratch_of(weights, image_rows, out_rows, width, extra=()):
    return [
        pltpu.VMEM((3, weights.blocks, weights.shape.m, weights.shape.cols_of, weights.shape.lanes), BF16),
        pltpu.VMEM((image_rows, width, weights.width), BF16),
        pltpu.VMEM((out_rows * width, weights.c_out), F32),
        pltpu.SemaphoreType.DMA((3, 8 * weights.blocks)),
    ] + list(extra)


def call(body, name, n_smem, n_vmem, n_any, outs, scratch, flops, limit=24 * 1024 * 1024):
    specs = (
        [pl.BlockSpec(memory_space=pltpu.SMEM)] * n_smem
        + [pl.BlockSpec(memory_space=pltpu.VMEM)] * n_vmem
        + [pl.BlockSpec(memory_space=pl.ANY)] * n_any
    )
    return pl.pallas_call(
        body,
        out_shape=[jax.ShapeDtypeStruct(s, d) for s, d in outs],
        in_specs=specs,
        out_specs=[pl.BlockSpec(memory_space=pltpu.VMEM)] * len(outs),
        scratch_shapes=scratch,
        compiler_params=pltpu.CompilerParams(vmem_limit_bytes=limit),
        cost_estimate=pl.CostEstimate(flops=flops, bytes_accessed=4_000_000, transcendentals=0),
        name=name,
    )


def message_outs(rows, width, channels, keep):
    return [
        ((rows * width + TAIL, channels), BF16),
        ((keep * width + TAIL, channels), BF16),
        ((keep * width, channels), BF16),
        ((8, channels), F32),
    ]


def prepare(shape, flags, x, keep):
    rows, width, c = shape.rows, shape.cols, shape.narrow

    def body(flags, x_ref, out_ref, outer_ref, inner_ref, stats_ref):
        out_ref[0 : rows * width, :] = x_ref[...]
        sums = moments_of(x_ref[...].astype(F32))
        emit(flags, out_ref, outer_ref, inner_ref, stats_ref, keep, rows, width, sums)

    return call(body, "prepare", 1, 1, 0, message_outs(rows, width, c, keep), [], 1000)(flags, x)


def fine_conv(shape, flags, weights, pieces, got, halo, out_halo, keep, residual=None, name="fine"):
    rows, width, half, c = shape.rows, shape.cols, shape.half, shape.narrow
    out_rows = rows + 2 * out_halo
    image_rows = out_rows + 2
    n_pieces = len(pieces)
    extra = 0 if residual is None else 3

    def body(flags, block, outer, inner, sa, sb, *rest):
        res = rest[:extra]
        piece_refs = rest[extra : extra + n_pieces]
        rest = rest[extra + n_pieces :]
        outs = rest[:-4]
        buffer, image, acc, sems = rest[-4:]
        copies = weights.copies(flags, weights.stacks(piece_refs), buffer, sems)
        for mine in copies:
            for copy in mine:
                copy.start()
        weights.clear(image)
        mean, inv = group_terms(sa[...] + sb[...], shape.fine_count)
        mix = parity_matrix(c)

        def store(row, place, size, tap, value):
            weights.put(image, row, place, tap, value.astype(BF16))

        for row in range(image_rows):
            value, outside = ext_row(row + halo - out_halo - 1, block, outer, inner, flags, rows, halo, width)
            value = masked(silu((value - mean) * inv), outside).astype(BF16)
            value = jnp.dot(value, mix, preferred_element_type=F32)
            fine_columns(store, row, width, value[:half], value[half:])
        run_conv(weights, buffer, image, acc, copies, out_rows, width)
        scale = 1.0 / math.sqrt(9 * c)
        if residual is None:
            out_ref, outer_ref, inner_ref, stats_ref = outs
            value = (acc[...] * scale).astype(BF16)
            out_ref[0 : rows * width, :] = value
            emit(flags, out_ref, outer_ref, inner_ref, stats_ref, keep, rows, width, moments_of(value.astype(F32)))
        else:
            (out_ref,) = outs
            for row in range(out_rows):
                own, _ = ext_row(row, res[0], res[1], res[2], flags, rows, out_halo, width)
                span = slice(row * width, (row + 1) * width)
                out_ref[span, :] = (own + acc[span, :] * scale).astype(BF16)

    outs = message_outs(rows, width, c, keep) if residual is None else [((out_rows * width, c), BF16)]
    args = (flags,) + tuple(got) + (() if residual is None else tuple(residual)) + tuple(pieces)
    flops = 2 * out_rows * width * 9 * c * c
    return call(body, name, 1, 5 + extra, n_pieces, outs, scratch_of(weights, image_rows, out_rows, width), flops)(*args)


def down_conv(shape, flags, weights, pieces, skip, keep):
    rows, width, half, c = shape.rows, shape.cols, shape.half, shape.narrow
    out_rows = rows // 2

    def body(flags, skip_ref, *rest):
        piece_refs = rest[: len(pieces)]
        outs = rest[len(pieces) : -4]
        buffer, image, acc, sems = rest[-4:]
        copies = weights.copies(flags, weights.stacks(piece_refs), buffer, sems)
        for mine in copies:
            for copy in mine:
                copy.start()
        weights.clear(image)
        for row in range(rows + 1):
            value = skip_ref[row * width : (row + 1) * width, :].astype(F32)
            if row == 0:
                value = masked(value, flags[1] != 0)
            even, odd = value[:half], value[half:]
            place = (row % 2) * (out_rows + 1) + row // 2
            weights.put(image, place, 0, 0, shifted(odd, 1).astype(BF16))
            weights.put(image, place, 0, 1, even.astype(BF16))
            weights.put(image, place, 0, 2, odd.astype(BF16))
        for dy in range(3):
            for copy in copies[dy]:
                copy.wait()
            begin = (0, out_rows + 1, 1)[dy]
            left = image[begin : begin + out_rows].reshape(out_rows * half, weights.width)
            made = weights.product(left, buffer, dy)
            if dy == 0:
                acc[...] = made
            else:
                acc[...] += made
        out_ref, outer_ref, inner_ref, stats_ref = outs
        value = (acc[...] * (1.0 / math.sqrt(9 * c))).astype(BF16)
        out_ref[0 : out_rows * half, :] = value
        emit(flags, out_ref, outer_ref, inner_ref, stats_ref, keep, out_rows, half, moments_of(value.astype(F32)))

    scratch = scratch_of(weights, 2 * (out_rows + 1), out_rows, half)
    outs = message_outs(out_rows, half, shape.wide, keep)
    return call(body, "down", 1, 1, len(pieces), outs, scratch, 2 * out_rows * half * 9 * c * shape.wide)(flags, skip, *pieces)


def coarse_conv(shape, flags, weights, pieces, got, keep, residual=None, name="coarse"):
    rows, width, c = shape.rows // 2, shape.half, shape.wide
    extra = 0 if residual is None else 1

    def body(flags, block, outer, inner, sa, sb, *rest):
        res = rest[:extra]
        piece_refs = rest[extra : extra + len(pieces)]
        outs = rest[extra + len(pieces) : -4]
        buffer, image, acc, sems = rest[-4:]
        copies = weights.copies(flags, weights.stacks(piece_refs), buffer, sems)
        for mine in copies:
            for copy in mine:
                copy.start()
        weights.clear(image)
        mean, inv = group_terms(sa[...] + sb[...], shape.coarse_count)
        for row in range(rows + 2):
            value, outside = ext_row(row, block, outer, inner, flags, rows, 1, width)
            value = masked(silu((value - mean) * inv), outside)
            weights.put(image, row, 0, 0, shifted(value, 1).astype(BF16))
            weights.put(image, row, 0, 1, value.astype(BF16))
            weights.put(image, row, 0, 2, shifted(value, -1).astype(BF16))
        run_conv(weights, buffer, image, acc, copies, rows, width)
        out_ref, outer_ref, inner_ref, stats_ref = outs
        value = acc[...] * (1.0 / math.sqrt(9 * c))
        if residual is not None:
            value = res[0][0 : rows * width, :].astype(F32) + value
        value = value.astype(BF16)
        out_ref[0 : rows * width, :] = value
        emit(flags, out_ref, outer_ref, inner_ref, stats_ref, keep, rows, width, moments_of(value.astype(F32)))

    args = (flags,) + tuple(got) + (() if residual is None else (residual,)) + tuple(pieces)
    outs = message_outs(rows, width, c, keep)
    flops = 2 * rows * width * 9 * c * c
    return call(body, name, 1, 5 + extra, len(pieces), outs, scratch_of(weights, rows + 2, rows, width), flops)(*args)


def up_conv(shape, flags, weights, pieces, got, skip, keep):
    rows, width, half = shape.rows, shape.cols, shape.half
    c, c_out = shape.wide, shape.narrow

    def body(flags, block, outer, inner, skip_ref, *rest):
        piece_refs = rest[: len(pieces)]
        outs = rest[len(pieces) : -4]
        buffer, image, acc, sems = rest[-4:]
        copies = weights.copies(flags, weights.stacks(piece_refs), buffer, sems)
        for mine in copies:
            for copy in mine:
                copy.start()
        weights.clear(image)
        mix = parity_matrix(c)
        for row in range(rows // 2 + 2):
            value, outside = ext_row(row, block, outer, inner, flags, rows // 2, 1, half)
            value = masked(value, outside).astype(BF16)
            value = jnp.dot(value, mix, preferred_element_type=F32)
            before, after = shifted(value, 1).astype(BF16), shifted(value, -1).astype(BF16)
            value = value.astype(BF16)
            for fine in (2 * row - 1, 2 * row):
                if 0 <= fine < rows + 2:
                    for tap, (even, odd) in enumerate(((before, value), (value, value), (value, after))):
                        weights.put(image, fine, 0, tap, even)
                        weights.put(image, fine, half, tap, odd)
        run_conv(weights, buffer, image, acc, copies, rows, width)
        out_ref, outer_ref, inner_ref, stats_ref, skip_stats_ref = outs
        value = (acc[...] * (1.0 / math.sqrt(9 * c))).astype(BF16)
        out_ref[0 : rows * width, :] = value
        emit(flags, out_ref, outer_ref, inner_ref, stats_ref, keep, rows, width, moments_of(value.astype(F32)))
        own = skip_ref[width : (rows + 1) * width, :].astype(F32)
        skip_stats_ref[...] = row_stack(moments_of(own), 8, c_out)

    outs = message_outs(rows, width, c_out, keep) + [((8, c_out), F32)]
    flops = 2 * rows * width * 9 * c * c_out
    scratch = scratch_of(weights, rows + 2, rows, width)
    return call(body, "up", 1, 4, len(pieces), outs, scratch, flops)(flags, *got, skip, *pieces)


def join_conv(shape, flags, weights, pieces, got, skip, skip_sums, keep):
    rows, width, half, c = shape.rows, shape.cols, shape.half, shape.narrow

    def body(flags, block, outer, inner, sa, sb, skip_ref, skip_sum, *rest):
        piece_refs = rest[: len(pieces)]
        outs = rest[len(pieces) : -4]
        buffer, image, acc, sems = rest[-4:]
        copies = weights.copies(flags, weights.stacks(piece_refs), buffer, sems)
        for mine in copies:
            for copy in mine:
                copy.start()
        weights.clear(image)
        mix = parity_matrix(c)
        for part in range(2):
            sums = sa[...] + sb[...] if part == 0 else skip_sum[...]
            mean, inv = pair_terms(sums, shape.fine_count)

            def store(row, place, size, tap, value, part=part):
                weights.put(image, row, place, tap, value.astype(BF16), first=part * c)

            for row in range(rows + 2):
                if part == 0:
                    value, outside = ext_row(row, block, outer, inner, flags, rows, 1, width)
                else:
                    value = skip_ref[row * width : (row + 1) * width, :].astype(F32)
                    outside = flags[1] != 0 if row == 0 else flags[2] != 0 if row == rows + 1 else None
                value = masked(silu((value - mean) * inv), outside).astype(BF16)
                value = jnp.dot(value, mix, preferred_element_type=F32)
                fine_columns(store, row, width, value[:half], value[half:])
        run_conv(weights, buffer, image, acc, copies, rows, width)
        out_ref, outer_ref, inner_ref, stats_ref = outs
        value = (acc[...] * (1.0 / math.sqrt(18 * c))).astype(BF16)
        out_ref[0 : rows * width, :] = value
        emit(flags, out_ref, outer_ref, inner_ref, stats_ref, keep, rows, width, moments_of(value.astype(F32)))

    outs = message_outs(rows, width, c, keep)
    flops = 2 * rows * width * 18 * c * c
    scratch = scratch_of(weights, rows + 2, rows, width)
    return call(body, "join", 1, 7, len(pieces), outs, scratch, flops)(flags, *got, skip, skip_sums, *pieces)


def pair_terms(sums, count):
    width = sums.shape[1]
    size = 2 * width // GROUPS
    terms = row_stack(bf16_terms(sums[0:1]) + bf16_terms(sums[1:2]), 16, width).astype(BF16)
    left = lax.broadcasted_iota(jnp.int32, (width, width), 0) // size
    right = lax.broadcasted_iota(jnp.int32, (width, width), 1) // size
    together = jnp.where(left == right, 1.0, 0.0).astype(BF16)
    summed = jnp.dot(terms, together, preferred_element_type=F32) * (1.0 / (count * size))
    mean = summed[0:1] + summed[1:2] + summed[2:3]
    square = summed[3:4] + summed[4:5] + summed[5:6]
    variance = jnp.maximum(square - mean * mean, 0.0)
    return mean, lax.rsqrt(variance + EPSILON)


def last_conv(shape, flags, weights, pieces, got, u, skip, j_start, n_quarters):
    rows, width, half, c = shape.rows, shape.cols, shape.half, shape.narrow
    quarter = half // n_quarters
    j_block = j_start // shape.blk

    def body(flags, block, outer, inner, sa, sb, u_ref, skip_ref, *rest):
        piece_refs = rest[: len(pieces)]
        outs = rest[len(pieces) : -6]
        buffer, image, acc, sems, jbuf, jsem = rest[-6:]
        copies = weights.copies(flags, weights.stacks(piece_refs), buffer, sems)
        for mine in copies:
            for copy in mine:
                copy.start()
        weights.clear(image)
        jcopies = []
        for low, high, owners in weights.bounds:
            if low <= j_block < high:
                for ref, owner in zip(weights.stacks(piece_refs)[low], owners, strict=True):
                    for j in range(ref.shape[0]):
                        copy = pltpu.make_async_copy(
                            ref.at[j, j_block - low], jbuf.at[owner(flags, j)], jsem.at[len(jcopies)]
                        )
                        copy.start()
                        jcopies.append(copy)
        mean, inv = group_terms(sa[...] + sb[...], shape.fine_count)
        mix = parity_matrix(c)

        def store(row, place, size, tap, value):
            weights.put(image, row, place, tap, value.astype(BF16))

        for row in range(rows + 2):
            value, outside = ext_row(row, block, outer, inner, flags, rows, 1, width)
            value = masked(silu((value - mean) * inv), outside).astype(BF16)
            value = jnp.dot(value, mix, preferred_element_type=F32)
            fine_columns(store, row, width, value[:half], value[half:])
        run_conv(weights, buffer, image, acc, copies, rows, width)
        for copy in jcopies:
            copy.wait()
        right = jbuf[...].reshape(2 * c, shape.lanes)
        left = [u_ref[0 : rows * width, :], skip_ref[width : (rows + 1) * width, :]]
        left = [jnp.dot(part, mix, preferred_element_type=F32).astype(BF16) for part in left]
        made = jnp.zeros((rows * width, c), F32)
        for odd in range(2):
            mine = jnp.concatenate(
                [part[:, odd * (c // 2) : (odd + 1) * (c // 2)] for part in left]
                + [jnp.zeros((rows * width, shape.lanes - c), BF16)],
                axis=1,
            )
            made += lax.dot_general(
                mine, right[odd * c : (odd + 1) * c], (((1,), (1,)), ((), ())), preferred_element_type=F32
            )
        value = made * (1.0 / math.sqrt(2 * c)) + acc[...] * (1.0 / math.sqrt(9 * c))
        value = value.reshape(2 * rows, half, c).astype(BF16)
        for q, out in enumerate(outs):
            out[...] = value[:, q * quarter : (q + 1) * quarter, :]

    outs = [((2 * rows, quarter, c), BF16)] * n_quarters
    flops = 2 * rows * width * 11 * c * c
    extra = [pltpu.VMEM((shape.m, shape.cols_of, shape.lanes), BF16), pltpu.SemaphoreType.DMA((8,))]
    scratch = scratch_of(weights, rows + 2, rows, width, extra)
    return call(body, "last", 1, 7, len(pieces), outs, scratch, flops)(flags, *got, u, skip, *pieces)


def pack_blocks(shape, pack, low, high):
    count, columns = high - low, pack.shape[1]

    def body(pack_ref, out_ref, rows, sem):
        copy = pltpu.make_async_copy(pack_ref.at[low * shape.blk : high * shape.blk, :], rows, sem)
        copy.start()
        left = lax.broadcasted_iota(jnp.int32, (columns, columns), 0)
        right = lax.broadcasted_iota(jnp.int32, (columns, columns), 1)
        same = jnp.where(left == right, 1.0, 0.0).astype(BF16)
        copy.wait()
        for block in range(count):
            part = rows[block * shape.blk : (block + 1) * shape.blk, :]
            made = lax.dot_general(same, part, (((1,), (1,)), ((), ())), preferred_element_type=F32)
            out_ref[block, :, 0 : shape.blk] = made.astype(BF16)
            out_ref[block, :, shape.blk :] = jnp.zeros((columns, shape.lanes - shape.blk), BF16)

    scratch = [pltpu.VMEM((count * shape.blk, columns), BF16), pltpu.SemaphoreType.DMA(())]
    outs = [((count, columns, shape.lanes), BF16)]
    return call(body, f"pack{low}", 0, 0, 1, outs, scratch, 1000, 16 * 1024 * 1024)(pack)[0]


def shards(n, n_section, features, section_packs):
    section_id = lax.axis_index("section")
    w = lax.axis_index("space")
    shape = Shape(features, section_packs, n)
    q_rows = shape.narrow * shape.narrow // shape.wide
    pack = section_packs[0]
    flags = jnp.stack([w % 2, (w == 0).astype(jnp.int32), (w == n - 1).astype(jnp.int32), section_id, w]).astype(jnp.int32)

    total = pack.shape[0] // shape.blk
    cuts = [0, 9 * q_rows // shape.blk, 18 * q_rows // shape.blk, 36 * q_rows // shape.blk, total]
    bounds = list(zip(cuts[:-1], cuts[1:], strict=True))

    def permute(value, source, target, move):
        pairs = [(source * n + i, target * n + move(i)) for i in range(n)]
        return lax.ppermute(value, ("section", "space"), pairs)

    def to_outer(i):
        return (i + 1) % n if i % 2 else (i - 1) % n

    def ahead(i):
        return (i - 2) % n if i % 2 else (i + 2) % n

    def across(i):
        return (i + 4) % n

    def partner(i):
        return i ^ 1

    def sums_of(tail):
        tail = tail.astype(F32)
        first = tail[0:1] + tail[1:2] + tail[2:3]
        second = tail[3:4] + tail[4:5] + tail[5:6]
        return jnp.concatenate([first, second, jnp.zeros((6, tail.shape[1]), F32)], 0)

    def exchange(made, source, target, extra_stats=None, with_stats=True):
        block, outer, inner, stats = made
        if source != target:
            block = permute(block, source, target, lambda i: i)
            stats = None
        outer = permute(outer, source, target, to_outer)
        inner = permute(inner, source, target, partner)
        if not with_stats:
            return block, outer, inner
        own = made[3] if stats is not None else sums_of(block[-TAIL:])
        size = own.shape[1]
        sent = made[3] if extra_stats is None else jnp.concatenate([made[3], extra_stats], 1)
        if n == 8:
            b = permute(sent, source, target, ahead)
            c = permute(sent, source, target, across)
            if extra_stats is None:
                near = sums_of(outer[-TAIL:])
            else:
                own = sent
                near = permute(sent, source, target, to_outer)
            mine = own + near + b + c
            other = permute(mine, target, target, partner)
        else:
            mine = lax.psum(sent if stats is not None else own, "space")
            other = jnp.zeros_like(mine)
        if extra_stats is None:
            return block, outer, inner, mine, other
        total = mine[:, size:] + other[:, size:]
        return (block, outer, inner, mine[:, :size], other[:, :size]), total

    def within(value, planes, move):
        pairs = [(s * n + i, s * n + move(i)) for s in planes for i in range(n)]
        return lax.ppermute(value, ("section", "space"), pairs)

    def owner_near(flags, j):
        return ((flags[4] // 2) ^ j) * 2 + flags[0]

    def owner_far(flags, j):
        return ((flags[4] // 2) ^ j) * 2 + 1 - flags[0]

    pieces = []
    previous = None
    for number, (low, high) in enumerate(bounds):
        if n == 8:
            planes = range(n_section) if number < 3 else range(1, n_section)
            own = pack_blocks(shape, pack, low, high)
            if previous is not None:
                own, _ = lax.optimization_barrier((own, previous))
            got = [within(own, planes, lambda i, k=k: i ^ (2 * k)) for k in range(1, 4)]
            previous = got
            near = jnp.stack([own] + got)
            far = within(near, planes, partner)
            pieces.append(([near, far], [owner_near, owner_far]))
        else:
            got = lax.all_gather(pack[low * shape.blk : high * shape.blk], "space")
            got = got.reshape(shape.m, n // shape.m, high - low, shape.blk, -1).transpose(0, 2, 1, 4, 3)
            got = got.reshape(shape.m, high - low, shape.cols_of, shape.blk)
            got = jnp.pad(got, ((0, 0), (0, 0), (0, 0), (0, shape.lanes - shape.blk)))
            pieces.append(([got], [lambda flags, j: j]))

    def weights(start, c_in, c_out, parts):
        first = start // shape.blk
        end = (start + 9 * c_in * c_out // shape.wide) // shape.blk
        used = [i for i, (a, b) in enumerate(bounds) if a < end and b > first]
        made = Weights(shape, [bounds[i] + (pieces[i][1],) for i in used], start, c_in, c_out)
        return made, [stack for i in used for stack in pieces[i][0]]

    narrow, wide = shape.narrow, shape.wide
    x = features[0].reshape(shape.rows, shape.half, 2, narrow).transpose(0, 2, 1, 3).reshape(-1, narrow)
    first = exchange(prepare(shape, flags, x, 1), 0, 0)
    hidden = fine_conv(shape, flags, *weights(0, narrow, narrow, (narrow,)), first, 1, 0, 2, name="c00")
    second = exchange(hidden, 0, 0)
    (skip,) = fine_conv(
        shape, flags, *weights(9 * q_rows, narrow, narrow, (narrow,)), second, 2, 1, 0, residual=first[:3], name="c01"
    )
    coarse = down_conv(shape, flags, *weights(18 * q_rows, narrow, wide, (narrow,)), skip, 1)
    for section in (1, 2):
        got = exchange(coarse, section - 1, section)
        if section == 1:
            skip, got = lax.optimization_barrier((skip, got))
            skip = permute(skip, 0, 3, lambda i: i)
        hidden = coarse_conv(shape, flags, *weights(0, wide, wide, (wide,)), got, 1, name=f"c{section}0")
        then = exchange(hidden, section, section)
        coarse = coarse_conv(
            shape, flags, *weights(36 * q_rows, wide, wide, (wide,)), then, 1, residual=got[0], name=f"c{section}1"
        )
    got = exchange(coarse, 2, 3, with_stats=False)
    *up, skip_stats = up_conv(shape, flags, *weights(0, wide, narrow, (wide,)), got, skip, 1)
    got, skip_sums = exchange(up, 3, 3, extra_stats=skip_stats)
    hidden = join_conv(shape, flags, *weights(18 * q_rows, wide, narrow, (narrow, narrow)), got, skip, skip_sums, 1)
    then = exchange(hidden, 3, 3)
    outs = last_conv(
        shape, flags, *weights(36 * q_rows, narrow, narrow, (narrow,)), then, got[0], skip, 45 * q_rows, n_section
    )
    result = jnp.where(section_id == 3, outs[3], jnp.zeros_like(outs[3]))
    for target in range(3):
        result = result + permute(outs[target], 3, target, lambda i: i)
    quarter = shape.half // n_section
    result = result.reshape(shape.rows, 2, quarter, narrow).transpose(0, 2, 1, 3)
    return result.reshape(1, shape.rows, 2 * quarter, narrow)


def solution(mesh):
    n, n_section = mesh.shape["space"], mesh.shape["section"]

    def body(features, section_packs):
        return shards(n, n_section, features, section_packs)

    return jax.shard_map(
        body,
        mesh=mesh,
        in_specs=(P(None, "space", None, None), P("section", None, "space")),
        out_specs=P(None, "space", "section", None),
        check_vma=False,
    )
```

profile of v0, /device:TPU:16, one launch (start us, length us, event | category | flops | bytes accessed | tf_op | source)
XLA Modules:
  0.0 445.6 jit_solution(8719798677297018607)
XLA Ops:
  0.0 3.9 copy.12
  4.4 2.5 collective-permute-start.7
  8.5 5.8 %collective-permute-done.7 = bf16[3,80,512]{2,1,0:T(8,128)(2,1)S(1)} collective-permute-done((bf16[3,80,512]{2,1,0:T(8,128)(2,1)S(1)}, bf16[3,80,512]{2,1,0:T(8,128)(2,1)S(1)}, u32[]{:S(2)}, u32[]{:S(2)}) %collective-permute-start.7) | collective-permute-done | bytes 245792 | tf_op jit(solution)/shard_map/ppermute | solution.py:641
  14.3 4.1 collective-permute-done.6
  19.1 1.7 collective-permute-start.16
  20.8 1.2 collective-permute-start.15
  23.4 5.5 %collective-permute-done.16 = bf16[3,80,512]{2,1,0:T(8,128)(2,1)S(1)} collective-permute-done((bf16[3,80,512]{2,1,0:T(8,128)(2,1)S(1)}, bf16[3,80,512]{2,1,0:T(8,128)(2,1)S(1)}, u32[]{:S(2)}, u32[]{:S(2)}) %collective-permute-start.16) | collective-permute-done | bytes 245792 | tf_op jit(solution)/shard_map/ppermute | solution.py:641
  28.9 4.3 collective-permute-done.15
  33.2 1.4 collective-permute-start.20
  34.7 1.5 collective-permute-start.19
  36.7 2.0 pack12.1
  38.8 9.5 %collective-permute-done.20 = bf16[6,80,512]{2,1,0:T(8,128)(2,1)S(1)} collective-permute-done((bf16[6,80,512]{2,1,0:T(8,128)(2,1)S(1)}, bf16[6,80,512]{2,1,0:T(8,128)(2,1)S(1)}, u32[]{:S(2)}, u32[]{:S(2)}) %collective-permute-start.20) | collective-permute-done | bytes 491552 | tf_op jit(solution)/shard_map/ppermute | solution.py:641
  48.3 9.5 %collective-permute-done.19 = bf16[6,80,512]{2,1,0:T(8,128)(2,1)S(1)} collective-permute-done((bf16[6,80,512]{2,1,0:T(8,128)(2,1)S(1)}, bf16[6,80,512]{2,1,0:T(8,128)(2,1)S(1)}, u32[]{:S(2)}, u32[]{:S(2)}) %collective-permute-start.19) | collective-permute-done | bytes 491552 | tf_op jit(solution)/shard_map/ppermute | solution.py:641
  57.9 6.1 %collective-permute-start.35 = (bf16[12,80,512]{2,1,0:T(8,128)(2,1)}, bf16[12,80,512]{2,1,0:T(8,128)(2,1)}, u32[]{:S(2)}, u32[]{:S(2)}) collective-permute-start(bf16[12,80,512]{2,1,0:T(8,128)(2,1)} %pack12.1), channel_id=1, source_target_pairs={{8,14},{9,15},{10,12},{11,13},{12,10},{13,11},{14,8},{15,9},{16,22... | collective-permute-start | bytes 2949128 | tf_op jit(solution)/shard_map/ppermute | solution.py:641
  64.0 7.0 %collective-permute-start.34 = (bf16[12,80,512]{2,1,0:T(8,128)(2,1)}, bf16[12,80,512]{2,1,0:T(8,128)(2,1)}, u32[]{:S(2)}, u32[]{:S(2)}) collective-permute-start(bf16[12,80,512]{2,1,0:T(8,128)(2,1)} %pack12.1), channel_id=1, source_target_pairs={{8,12},{9,13},{10,14},{11,15},{12,8},{13,9},{14,10},{15,11},{16,20... | collective-permute-start | bytes 2949128 | tf_op jit(solution)/shard_map/ppermute | solution.py:641
  71.0 7.0 %collective-permute-start.33 = (bf16[12,80,512]{2,1,0:T(8,128)(2,1)}, bf16[12,80,512]{2,1,0:T(8,128)(2,1)}, u32[]{:S(2)}, u32[]{:S(2)}) collective-permute-start(bf16[12,80,512]{2,1,0:T(8,128)(2,1)} %pack12.1), channel_id=1, source_target_pairs={{8,10},{9,11},{10,8},{11,9},{12,14},{13,15},{14,12},{15,13},{16,18... | collective-permute-start | bytes 2949128 | tf_op jit(solution)/shard_map/ppermute | solution.py:641
  78.1 1.2 copy.10
  81.6 1.4 pad_maximum_fusion.2.rest_0_
  83.1 1.6 pad_maximum_fusion.1.rest_0_.rest_4_
  84.6 4.7 %collective-permute-done.35 = bf16[12,80,512]{2,1,0:T(8,128)(2,1)} collective-permute-done((bf16[12,80,512]{2,1,0:T(8,128)(2,1)}, bf16[12,80,512]{2,1,0:T(8,128)(2,1)}, u32[]{:S(2)}, u32[]{:S(2)}) %collective-permute-start.35) | collective-permute-done | bytes 983072 | tf_op jit(solution)/shard_map/ppermute | solution.py:641
  90.0 19.8 %collective-permute-done.34 = bf16[12,80,512]{2,1,0:T(8,128)(2,1)} collective-permute-done((bf16[12,80,512]{2,1,0:T(8,128)(2,1)}, bf16[12,80,512]{2,1,0:T(8,128)(2,1)}, u32[]{:S(2)}, u32[]{:S(2)}) %collective-permute-start.34) | collective-permute-done | bytes 983072 | tf_op jit(solution)/shard_map/ppermute | solution.py:641
  109.8 3.9 collective-permute-start.8
  113.7 5.7 %collective-permute-start.21 = (bf16[4,6,80,512]{3,2,1,0:T(8,128)(2,1)S(1)}, bf16[4,6,80,512]{3,2,1,0:T(8,128)(2,1)S(1)}, u32[]{:S(2)}, u32[]{:S(2)}) collective-permute-start(bf16[4,6,80,512]{3,2,1,0:T(8,128)(2,1)S(1)} %pad_maximum_fusion.1.rest_0_.rest_4_), channel_id=1, source_target_pairs={{0,1},{1,0},{2,3},{3,2},{4,5},{5,4},{6,7},{7,6},{8,9},{9,8},{10,11... | collective-permute-start | bytes 5898248 | tf_op jit(solution)/shard_map/ppermute | solution.py:641
  119.4 2.4 pad_maximum_fusion.rest_1_.rest_0_
  121.9 7.0 %collective-permute-start.36 = (bf16[4,12,80,512]{3,2,1,0:T(8,128)(2,1)S(1)}, bf16[4,12,80,512]{3,2,1,0:T(8,128)(2,1)S(1)}, u32[]{:S(2)}, u32[]{:S(2)}) collective-permute-start(bf16[4,12,80,512]{3,2,1,0:T(8,128)(2,1)S(1)} %pad_maximum_fusion.rest_1_.rest_0_), channel_id=1, source_target_pairs={{8,9},{9,8},{10,11},{11,10},{12,13},{13,12},{14,15},{15,14},{16,17... | collective-permute-start | bytes 11796488 | tf_op jit(solution)/shard_map/ppermute | solution.py:641
  129.8 5.8 %collective-permute-start.17 = (bf16[4,3,80,512]{3,2,1,0:T(8,128)(2,1)S(1)}, bf16[4,3,80,512]{3,2,1,0:T(8,128)(2,1)S(1)}, u32[]{:S(2)}, u32[]{:S(2)}) collective-permute-start(bf16[4,3,80,512]{3,2,1,0:T(8,128)(2,1)S(1)} %pad_maximum_fusion.3.rest_3_.rest_2_), channel_id=1, source_target_pairs={{0,1},{1,0},{2,3},{3,2},{4,5},{5,4},{6,7},{7,6},{8,9},{9,8},{10,11... | collective-permute-start | bytes 2949128 | tf_op jit(solution)/shard_map/ppermute | solution.py:641
  136.4 7.0 %c00.1 = (bf16[528,320]{1,0:T(8,128)(2,1)S(1)}, bf16[272,320]{1,0:T(8,128)(2,1)S(1)}, bf16[256,320]{1,0:T(8,128)(2,1)S(1)}, f32[8,320]{1,0:T(8,128)S(1)}) custom-call(s32[5]{0:T(128)S(1)} %stack.91.flags, bf16[528,320]{1,0:T(8,128)(2,1)S(1)} %get-tuple-element.54.block.rest_0_, bf16[144,320]{1,0:T(8,128)(2,1)S(1)} %collective-permute-done.outer.rest_1_, ...), custom_call_target="tpu_custom_call" | custom-call | flops 943718400 | bytes 4000000 | tf_op jit(solution)/shard_map/c00/pallas_call | solution.py:316
  147.1 8.0 %c01.1.skip_ref = bf16[768,320]{1,0:T(8,128)(2,1)S(1)} custom-call(s32[5]{0:T(128)S(1)} %stack.91.flags, bf16[528,320]{1,0:T(8,128)(2,1)S(1)} %get-tuple-element.58.block, bf16[272,320]{1,0:T(8,128)(2,1)S(1)} %collective-permute-done.9.outer, bf16[256,320]{1,0:T(8,128)(2,1)S(1)} %collective-permute-done.10.inner, f32[8,320]{1,0:T(8,128)S(1)} %fusion.11.sa, ...), custom_call_target="tpu_custom_call" | custom-call | flops 1415577600 | bytes 4000000 | tf_op jit(solution)/shard_map/c01/pallas_call | solution.py:316
  155.1 8.1 %down.1 = (bf16[144,640]{1,0:T(8,128)(2,1)S(1)}, bf16[80,640]{1,0:T(8,128)(2,1)S(1)}, bf16[64,640]{1,0:T(8,128)(2,1)S(1)}, f32[8,640]{1,0:T(8,128)S(1)}) custom-call(s32[5]{0:T(128)S(1)} %stack.91.flags, bf16[768,320]{1,0:T(8,128)(2,1)S(1)} %c01.1.skip_ref, bf16[4,6,80,512]{3,2,1,0:T(8,128)(2,1)S(1)} %pad_maximum_fusion.1.rest_0_.rest_4_, ...), custom_call_target="tpu_custom_call" | custom-call | flops 471859200 | bytes 4000000 | tf_op jit(solution)/shard_map/down/pallas_call | solution.py:358
  167.4 15.6 %c10.1 = (bf16[144,640]{1,0:T(8,128)(2,1)S(1)}, bf16[80,640]{1,0:T(8,128)(2,1)S(1)}, bf16[64,640]{1,0:T(8,128)(2,1)S(1)}, f32[8,640]{1,0:T(8,128)S(1)}) custom-call(s32[5]{0:T(128)S(1)} %stack.91.flags, bf16[144,640]{1,0:T(8,128)(2,1)S(1)} %collective-permute-done.22.block.rest_0_, bf16[80,640]{1,0:T(8,128)(2,1)S(1)} %collective-permute-done.23.outer, ...), custom_call_target="tpu_custom_call" | custom-call | flops 943718400 | bytes 4000000 | tf_op jit(solution)/shard_map/c10/pallas_call | solution.py:394
  187.0 15.6 %c11.1 = (bf16[144,640]{1,0:T(8,128)(2,1)S(1)}, bf16[80,640]{1,0:T(8,128)(2,1)S(1)}, bf16[64,640]{1,0:T(8,128)(2,1)S(1)}, f32[8,640]{1,0:T(8,128)S(1)}) custom-call(s32[5]{0:T(128)S(1)} %stack.91.flags, bf16[144,640]{1,0:T(8,128)(2,1)S(1)} %get-tuple-element.73.block, bf16[80,640]{1,0:T(8,128)(2,1)S(1)} %collective-permute-done.28.outer, ...), custom_call_target="tpu_custom_call" | custom-call | flops 943718400 | bytes 4000000 | tf_op jit(solution)/shard_map/c11/pallas_call | solution.py:394
  202.7 1.3 collective-permute-start.38
  204.0 1.3 collective-permute-start.41
  205.3 1.3 collective-permute-start.40
  206.6 1.3 collective-permute-start.39
  207.9 1.3 collective-permute-start.37
  209.2 40.4 %collective-permute-done.38.outer = bf16[80,640]{1,0:T(8,128)(2,1)S(1)} collective-permute-done((bf16[80,640]{1,0:T(8,128)(2,1)S(1)}, bf16[80,640]{1,0:T(8,128)(2,1)S(1)}, u32[]{:S(2)}, u32[]{:S(2)}) %collective-permute-start.38) | collective-permute-done | bytes 102432 | tf_op jit(solution)/shard_map/ppermute | solution.py:589
  249.6 18.2 %collective-permute-done.37.block.rest_0_ = bf16[144,640]{1,0:T(8,128)(2,1)S(1)} collective-permute-done((bf16[144,640]{1,0:T(8,128)(2,1)S(1)}, bf16[144,640]{1,0:T(8,128)(2,1)S(1)}, u32[]{:S(2)}, u32[]{:S(2)}) %collective-permute-start.37) | collective-permute-done | bytes 184352 | tf_op jit(solution)/shard_map/ppermute | solution.py:589
  267.9 1.9 collective-permute-start.42
  269.9 1.1 collective-permute-done.42.sb
  271.0 16.3 %c20.1 = (bf16[144,640]{1,0:T(8,128)(2,1)S(1)}, bf16[80,640]{1,0:T(8,128)(2,1)}, bf16[64,640]{1,0:T(8,128)(2,1)S(1)}, f32[8,640]{1,0:T(8,128)S(1)}) custom-call(s32[5]{0:T(128)S(1)} %stack.91.flags, bf16[144,640]{1,0:T(8,128)(2,1)S(1)} %collective-permute-done.37.block.rest_0_, bf16[80,640]{1,0:T(8,128)(2,1)S(1)} %collective-permute-done.38.outer, ...), custom_call_target="tpu_custom_call" | custom-call | flops 943718400 | bytes 4000000 | tf_op jit(solution)/shard_map/c20/pallas_call | solution.py:394
  289.2 1.9 collective-permute-start.43
  292.2 1.5 collective-permute-start.51
  293.7 3.5 collective-permute-start.46
  297.2 3.7 collective-permute-start.45
  300.9 2.6 collective-permute-start.44
  305.1 1.9 collective-permute-start.47
  308.1 2.1 copy-done.1
  310.3 2.1 copy-done.4
  314.2 16.7 %c21.1 = (bf16[144,640]{1,0:T(8,128)(2,1)}, bf16[80,640]{1,0:T(8,128)(2,1)}, bf16[64,640]{1,0:T(8,128)(2,1)}, f32[8,640]{1,0:T(8,128)}) custom-call(s32[5]{0:T(128)S(1)} %stack.91.flags, bf16[144,640]{1,0:T(8,128)(2,1)S(1)} %copy-done.20, bf16[80,640]{1,0:T(8,128)(2,1)} %collective-permute-done.43.outer, bf16[64,640]{1,0:T(8,128)(2,1)S(1)} %collective-permute-done.44.inner, ...), custom_call_target="tpu_custom_call" | custom-call | flops 943718400 | bytes 4000000 | tf_op jit(solution)/shard_map/c21/pallas_call | solution.py:394
  330.9 2.0 collective-permute-start.48
  332.9 5.4 %collective-permute-start.49 = (bf16[80,640]{1,0:T(8,128)(2,1)}, bf16[80,640]{1,0:T(8,128)(2,1)}, u32[]{:S(2)}, u32[]{:S(2)}) collective-permute-start(bf16[80,640]{1,0:T(8,128)(2,1)} %get-tuple-element.87), channel_id=1, source_target_pairs={{16,31},{17,26},{18,25},{19,28},{20,27},{21,30},{22,29},{23,24}} | collective-permute-start | bytes 307208 | tf_op jit(solution)/shard_map/ppermute | solution.py:589
  338.4 2.6 collective-permute-start.50
  341.0 1.3 copy.14.skip_ref
  343.1 1.2 copy-done.9
  344.3 1.2 copy-done.11
  345.5 1.2 copy-done.13
  346.7 12.2 %up.1 = (bf16[528,320]{1,0:T(8,128)(2,1)S(1)}, bf16[144,320]{1,0:T(8,128)(2,1)S(1)}, bf16[128,320]{1,0:T(8,128)(2,1)S(1)}, f32[8,320]{1,0:T(8,128)S(1)}, f32[8,320]{1,0:T(8,128)S(1)}) custom-call(s32[5]{0:T(128)S(1)} %stack.91.flags, bf16[144,640]{1,0:T(8,128)(2,1)} %collective-permute-done.48.block, bf16[80,640]{1,0:T(8,128)(2,1)} %collective-permute-done.49.outer, ...), custom_call_target="tpu_custom_call" | custom-call | flops 1887436800 | bytes 4000000 | tf_op jit(solution)/shard_map/up/pallas_call | solution.py:433
  363.2 12.3 %join.1 = (bf16[528,320]{1,0:T(8,128)(2,1)S(1)}, bf16[144,320]{1,0:T(8,128)(2,1)S(1)}, bf16[128,320]{1,0:T(8,128)(2,1)S(1)}, f32[8,320]{1,0:T(8,128)S(1)}) custom-call(s32[5]{0:T(128)S(1)} %stack.91.flags, bf16[528,320]{1,0:T(8,128)(2,1)S(1)} %get-tuple-element.90.block.u_ref, bf16[144,320]{1,0:T(8,128)(2,1)S(1)} %collective-permute-done.52.outer, ...), custom_call_target="tpu_custom_call" | custom-call | flops 1887436800 | bytes 4000000 | tf_op jit(solution)/shard_map/join/pallas_call | solution.py:474
  379.3 9.0 %last.1 = (bf16[8,16,320]{2,1,0:T(8,128)(2,1)S(1)}, bf16[8,16,320]{2,1,0:T(8,128)(2,1)S(1)}, bf16[8,16,320]{2,1,0:T(8,128)(2,1)S(1)}, bf16[8,16,320]{2,1,0:T(8,128)(2,1)S(1)}) custom-call(s32[5]{0:T(128)S(1)} %stack.91.flags, bf16[528,320]{1,0:T(8,128)(2,1)S(1)} %get-tuple-element.95.block, bf16[144,320]{1,0:T(8,128)(2,1)S(1)} %collective-permute-done.58.outer, ...), custom_call_target="tpu_custom_call" | custom-call | flops 1153433600 | bytes 4000000 | tf_op jit(solution)/shard_map/last/pallas_call | solution.py:551
  388.2 37.0 %collective-permute-start.63 = (bf16[8,16,320]{2,1,0:T(8,128)(2,1)S(1)}, bf16[8,16,320]{2,1,0:T(8,128)(2,1)S(1)}, u32[]{:S(2)}, u32[]{:S(2)}) collective-permute-start(bf16[8,16,320]{2,1,0:T(8,128)(2,1)S(1)} %get-tuple-element.100), channel_id=1, source_target_pairs={{24,0},{25,1},{26,2},{27,3},{28,4},{29,5},{30,6},{31,7}} | collective-permute-start | bytes 245768 | tf_op jit(solution)/shard_map/ppermute | solution.py:589
  425.3 7.0 %collective-permute-start.64 = (bf16[8,16,320]{2,1,0:T(8,128)(2,1)S(1)}, bf16[8,16,320]{2,1,0:T(8,128)(2,1)S(1)}, u32[]{:S(2)}, u32[]{:S(2)}) collective-permute-start(bf16[8,16,320]{2,1,0:T(8,128)(2,1)S(1)} %get-tuple-element.101), channel_id=1, source_target_pairs={{24,8},{25,9},{26,10},{27,11},{28,12},{29,13},{30,14},{31,15}} | collective-permute-start | bytes 245768 | tf_op jit(solution)/shard_map/ppermute | solution.py:589
  432.3 7.0 %collective-permute-start.65 = (bf16[8,16,320]{2,1,0:T(8,128)(2,1)S(1)}, bf16[8,16,320]{2,1,0:T(8,128)(2,1)S(1)}, u32[]{:S(2)}, u32[]{:S(2)}) collective-permute-start(bf16[8,16,320]{2,1,0:T(8,128)(2,1)S(1)} %get-tuple-element.102), channel_id=1, source_target_pairs={{24,16},{25,17},{26,18},{27,19},{28,20},{29,21},{30,22},{31,23}} | collective-permute-start | bytes 245768 | tf_op jit(solution)/shard_map/ppermute | solution.py:589
  439.3 5.2 %collective-permute-done.65 = bf16[8,16,320]{2,1,0:T(8,128)(2,1)S(1)} collective-permute-done((bf16[8,16,320]{2,1,0:T(8,128)(2,1)S(1)}, bf16[8,16,320]{2,1,0:T(8,128)(2,1)S(1)}, u32[]{:S(2)}, u32[]{:S(2)}) %collective-permute-start.65) | collective-permute-done | bytes 81952 | tf_op jit(solution)/shard_map/ppermute | solution.py:589
  (196 shorter events, 38.0 us)
Async XLA Ops:
  4.4 9.8 %collective-permute-start.7 = (bf16[3,80,512]{2,1,0:T(8,128)(2,1)S(1)}, bf16[3,80,512]{2,1,0:T(8,128)(2,1)S(1)}, u32[]{:S(2)}, u32[]{:S(2)}) collective-permute-start(bf16[3,80,512]{2,1,0:T(8,128)(2,1)S(1)} %pack0.1), channel_id=1, source_target_pairs={{0,6},{1,7},{2,4},{3,5},{4,2},{5,3},{6,0},{7,1},{8,14},{9,15},{10,... | collective-permute-start | bytes 737288 | tf_op jit(solution)/shard_map/ppermute | solution.py:641
  7.0 11.4 %collective-permute-start.6 = (bf16[3,80,512]{2,1,0:T(8,128)(2,1)S(1)}, bf16[3,80,512]{2,1,0:T(8,128)(2,1)S(1)}, u32[]{:S(2)}, u32[]{:S(2)}) collective-permute-start(bf16[3,80,512]{2,1,0:T(8,128)(2,1)S(1)} %pack0.1), channel_id=1, source_target_pairs={{0,4},{1,5},{2,6},{3,7},{4,0},{5,1},{6,2},{7,3},{8,12},{9,13},{10,... | collective-permute-start | bytes 737288 | tf_op jit(solution)/shard_map/ppermute | solution.py:641
  7.5 11.0 %collective-permute-start.5 = (bf16[3,80,512]{2,1,0:T(8,128)(2,1)S(1)}, bf16[3,80,512]{2,1,0:T(8,128)(2,1)S(1)}, u32[]{:S(2)}, u32[]{:S(2)}) collective-permute-start(bf16[3,80,512]{2,1,0:T(8,128)(2,1)S(1)} %pack0.1), channel_id=1, source_target_pairs={{0,2},{1,3},{2,0},{3,1},{4,6},{5,7},{6,4},{7,5},{8,10},{9,11},{10,... | collective-permute-start | bytes 737288 | tf_op jit(solution)/shard_map/ppermute | solution.py:641
  19.1 9.8 %collective-permute-start.16 = (bf16[3,80,512]{2,1,0:T(8,128)(2,1)S(1)}, bf16[3,80,512]{2,1,0:T(8,128)(2,1)S(1)}, u32[]{:S(2)}, u32[]{:S(2)}) collective-permute-start(bf16[3,80,512]{2,1,0:T(8,128)(2,1)S(1)} %pack3.1), channel_id=1, source_target_pairs={{0,6},{1,7},{2,4},{3,5},{4,2},{5,3},{6,0},{7,1},{8,14},{9,15},{10,... | collective-permute-start | bytes 737288 | tf_op jit(solution)/shard_map/ppermute | solution.py:641
  20.8 12.3 %collective-permute-start.15 = (bf16[3,80,512]{2,1,0:T(8,128)(2,1)S(1)}, bf16[3,80,512]{2,1,0:T(8,128)(2,1)S(1)}, u32[]{:S(2)}, u32[]{:S(2)}) collective-permute-start(bf16[3,80,512]{2,1,0:T(8,128)(2,1)S(1)} %pack3.1), channel_id=1, source_target_pairs={{0,4},{1,5},{2,6},{3,7},{4,0},{5,1},{6,2},{7,3},{8,12},{9,13},{10,... | collective-permute-start | bytes 737288 | tf_op jit(solution)/shard_map/ppermute | solution.py:641
  22.1 11.2 %collective-permute-start.14 = (bf16[3,80,512]{2,1,0:T(8,128)(2,1)S(1)}, bf16[3,80,512]{2,1,0:T(8,128)(2,1)S(1)}, u32[]{:S(2)}, u32[]{:S(2)}) collective-permute-start(bf16[3,80,512]{2,1,0:T(8,128)(2,1)S(1)} %pack3.1), channel_id=1, source_target_pairs={{0,2},{1,3},{2,0},{3,1},{4,6},{5,7},{6,4},{7,5},{8,10},{9,11},{10,... | collective-permute-start | bytes 737288 | tf_op jit(solution)/shard_map/ppermute | solution.py:641
  33.2 15.0 %collective-permute-start.20 = (bf16[6,80,512]{2,1,0:T(8,128)(2,1)S(1)}, bf16[6,80,512]{2,1,0:T(8,128)(2,1)S(1)}, u32[]{:S(2)}, u32[]{:S(2)}) collective-permute-start(bf16[6,80,512]{2,1,0:T(8,128)(2,1)S(1)} %pack6.1), channel_id=1, source_target_pairs={{0,6},{1,7},{2,4},{3,5},{4,2},{5,3},{6,0},{7,1},{8,14},{9,15},{10,... | collective-permute-start | bytes 1474568 | tf_op jit(solution)/shard_map/ppermute | solution.py:641
  34.7 23.1 %collective-permute-start.19 = (bf16[6,80,512]{2,1,0:T(8,128)(2,1)S(1)}, bf16[6,80,512]{2,1,0:T(8,128)(2,1)S(1)}, u32[]{:S(2)}, u32[]{:S(2)}) collective-permute-start(bf16[6,80,512]{2,1,0:T(8,128)(2,1)S(1)} %pack6.1), channel_id=1, source_target_pairs={{0,4},{1,5},{2,6},{3,7},{4,0},{5,1},{6,2},{7,3},{8,12},{9,13},{10,... | collective-permute-start | bytes 1474568 | tf_op jit(solution)/shard_map/ppermute | solution.py:641
  36.2 21.7 %collective-permute-start.18 = (bf16[6,80,512]{2,1,0:T(8,128)(2,1)S(1)}, bf16[6,80,512]{2,1,0:T(8,128)(2,1)S(1)}, u32[]{:S(2)}, u32[]{:S(2)}) collective-permute-start(bf16[6,80,512]{2,1,0:T(8,128)(2,1)S(1)} %pack6.1), channel_id=1, source_target_pairs={{0,2},{1,3},{2,0},{3,1},{4,6},{5,7},{6,4},{7,5},{8,10},{9,11},{10,... | collective-permute-start | bytes 1474568 | tf_op jit(solution)/shard_map/ppermute | solution.py:641
  57.9 31.4 %collective-permute-start.35 = (bf16[12,80,512]{2,1,0:T(8,128)(2,1)}, bf16[12,80,512]{2,1,0:T(8,128)(2,1)}, u32[]{:S(2)}, u32[]{:S(2)}) collective-permute-start(bf16[12,80,512]{2,1,0:T(8,128)(2,1)} %pack12.1), channel_id=1, source_target_pairs={{8,14},{9,15},{10,12},{11,13},{12,10},{13,11},{14,8},{15,9},{16,22... | collective-permute-start | bytes 2949128 | tf_op jit(solution)/shard_map/ppermute | solution.py:641
  64.0 45.8 %collective-permute-start.34 = (bf16[12,80,512]{2,1,0:T(8,128)(2,1)}, bf16[12,80,512]{2,1,0:T(8,128)(2,1)}, u32[]{:S(2)}, u32[]{:S(2)}) collective-permute-start(bf16[12,80,512]{2,1,0:T(8,128)(2,1)} %pack12.1), channel_id=1, source_target_pairs={{8,12},{9,13},{10,14},{11,15},{12,8},{13,9},{14,10},{15,11},{16,20... | collective-permute-start | bytes 2949128 | tf_op jit(solution)/shard_map/ppermute | solution.py:641
  71.0 42.7 %collective-permute-start.33 = (bf16[12,80,512]{2,1,0:T(8,128)(2,1)}, bf16[12,80,512]{2,1,0:T(8,128)(2,1)}, u32[]{:S(2)}, u32[]{:S(2)}) collective-permute-start(bf16[12,80,512]{2,1,0:T(8,128)(2,1)} %pack12.1), channel_id=1, source_target_pairs={{8,10},{9,11},{10,8},{11,9},{12,14},{13,15},{14,12},{15,13},{16,18... | collective-permute-start | bytes 2949128 | tf_op jit(solution)/shard_map/ppermute | solution.py:641
  80.2 48.9 %collective-permute-start.3 = (f32[8,320]{1,0:T(8,128)S(1)}, f32[8,320]{1,0:T(8,128)S(1)}, u32[]{:S(2)}, u32[]{:S(2)}) collective-permute-start(f32[8,320]{1,0:T(8,128)S(1)} %get-tuple-element.57), channel_id=1, source_target_pairs={{0,4},{1,5},{2,6},{3,7},{4,0},{5,1},{6,2},{7,3}} | collective-permute-start | bytes 30728 | tf_op jit(solution)/shard_map/ppermute | solution.py:589
  80.9 48.9 %collective-permute-start.2 = (f32[8,320]{1,0:T(8,128)S(1)}, f32[8,320]{1,0:T(8,128)S(1)}, u32[]{:S(2)}, u32[]{:S(2)}) collective-permute-start(f32[8,320]{1,0:T(8,128)S(1)} %get-tuple-element.57), channel_id=1, source_target_pairs={{0,2},{1,7},{2,4},{3,1},{4,6},{5,3},{6,0},{7,5}} | collective-permute-start | bytes 30728 | tf_op jit(solution)/shard_map/ppermute | solution.py:589
  89.3 32.5 %collective-permute-start = (bf16[144,320]{1,0:T(8,128)(2,1)S(1)}, bf16[144,320]{1,0:T(8,128)(2,1)S(1)}, u32[]{:S(2)}, u32[]{:S(2)}) collective-permute-start(bf16[144,320]{1,0:T(8,128)(2,1)S(1)} %get-tuple-element.55), channel_id=1, source_target_pairs={{0,7},{1,2},{2,1},{3,4},{4,3},{5,6},{6,5},{7,0}} | collective-permute-start | bytes 276488 | tf_op jit(solution)/shard_map/ppermute | solution.py:589
  109.8 26.6 %collective-permute-start.8 = (bf16[4,3,80,512]{3,2,1,0:T(8,128)(2,1)S(1)}, bf16[4,3,80,512]{3,2,1,0:T(8,128)(2,1)S(1)}, u32[]{:S(2)}, u32[]{:S(2)}) collective-permute-start(bf16[4,3,80,512]{3,2,1,0:T(8,128)(2,1)S(1)} %pad_maximum_fusion.2.rest_0_), channel_id=1, source_target_pairs={{0,1},{1,0},{2,3},{3,2},{4,5},{5,4},{6,7},{7,6},{8,9},{9,8},{10,11... | collective-permute-start | bytes 2949128 | tf_op jit(solution)/shard_map/ppermute | solution.py:641
  113.7 41.4 %collective-permute-start.21 = (bf16[4,6,80,512]{3,2,1,0:T(8,128)(2,1)S(1)}, bf16[4,6,80,512]{3,2,1,0:T(8,128)(2,1)S(1)}, u32[]{:S(2)}, u32[]{:S(2)}) collective-permute-start(bf16[4,6,80,512]{3,2,1,0:T(8,128)(2,1)S(1)} %pad_maximum_fusion.1.rest_0_.rest_4_), channel_id=1, source_target_pairs={{0,1},{1,0},{2,3},{3,2},{4,5},{5,4},{6,7},{7,6},{8,9},{9,8},{10,11... | collective-permute-start | bytes 5898248 | tf_op jit(solution)/shard_map/ppermute | solution.py:641
  121.9 65.1 %collective-permute-start.36 = (bf16[4,12,80,512]{3,2,1,0:T(8,128)(2,1)S(1)}, bf16[4,12,80,512]{3,2,1,0:T(8,128)(2,1)S(1)}, u32[]{:S(2)}, u32[]{:S(2)}) collective-permute-start(bf16[4,12,80,512]{3,2,1,0:T(8,128)(2,1)S(1)} %pad_maximum_fusion.rest_1_.rest_0_), channel_id=1, source_target_pairs={{8,9},{9,8},{10,11},{11,10},{12,13},{13,12},{14,15},{15,14},{16,17... | collective-permute-start | bytes 11796488 | tf_op jit(solution)/shard_map/ppermute | solution.py:641
  129.1 6.6 %collective-permute-start.1 = (bf16[128,320]{1,0:T(8,128)(2,1)S(1)}, bf16[128,320]{1,0:T(8,128)(2,1)S(1)}, u32[]{:S(2)}, u32[]{:S(2)}) collective-permute-start(bf16[128,320]{1,0:T(8,128)(2,1)S(1)} %get-tuple-element.56), channel_id=1, source_target_pairs={{0,1},{1,0},{2,3},{3,2},{4,5},{5,4},{6,7},{7,6}} | collective-permute-start | bytes 245768 | tf_op jit(solution)/shard_map/ppermute | solution.py:589
  129.8 17.3 %collective-permute-start.17 = (bf16[4,3,80,512]{3,2,1,0:T(8,128)(2,1)S(1)}, bf16[4,3,80,512]{3,2,1,0:T(8,128)(2,1)S(1)}, u32[]{:S(2)}, u32[]{:S(2)}) collective-permute-start(bf16[4,3,80,512]{3,2,1,0:T(8,128)(2,1)S(1)} %pad_maximum_fusion.3.rest_3_.rest_2_), channel_id=1, source_target_pairs={{0,1},{1,0},{2,3},{3,2},{4,5},{5,4},{6,7},{7,6},{8,9},{9,8},{10,11... | collective-permute-start | bytes 2949128 | tf_op jit(solution)/shard_map/ppermute | solution.py:641
  143.4 1.4 collective-permute-start.9
  144.0 1.4 collective-permute-start.12
  144.7 1.4 collective-permute-start.11
  145.4 1.6 collective-permute-start.10
  146.2 0.9 collective-permute-start.13
  163.2 2.7 collective-permute-start.23
  163.9 2.8 collective-permute-start.26
  164.5 2.1 collective-permute-start.25
  165.2 2.2 collective-permute-start.24
  165.9 0.7 collective-permute-start.22
  183.1 2.7 collective-permute-start.28
  183.7 2.1 collective-permute-start.31
  184.4 1.4 collective-permute-start.30
  185.1 1.9 collective-permute-start.29
  185.9 1.1 collective-permute-start.32
  202.7 46.9 %collective-permute-start.38 = (bf16[80,640]{1,0:T(8,128)(2,1)S(1)}, bf16[80,640]{1,0:T(8,128)(2,1)S(1)}, u32[]{:S(2)}, u32[]{:S(2)}) collective-permute-start(bf16[80,640]{1,0:T(8,128)(2,1)S(1)} %get-tuple-element.79), channel_id=1, source_target_pairs={{8,23},{9,18},{10,17},{11,20},{12,19},{13,22},{14,21},{15,16}} | collective-permute-start | bytes 307208 | tf_op jit(solution)/shard_map/ppermute | solution.py:589
  204.0 63.9 %collective-permute-start.41 = (f32[8,640]{1,0:T(8,128)S(1)}, f32[8,640]{1,0:T(8,128)S(1)}, u32[]{:S(2)}, u32[]{:S(2)}) collective-permute-start(f32[8,640]{1,0:T(8,128)S(1)} %get-tuple-element.81), channel_id=1, source_target_pairs={{8,20},{9,21},{10,22},{11,23},{12,16},{13,17},{14,18},{15,19}} | collective-permute-start | bytes 61448 | tf_op jit(solution)/shard_map/ppermute | solution.py:589
  205.3 62.6 %collective-permute-start.40 = (f32[8,640]{1,0:T(8,128)S(1)}, f32[8,640]{1,0:T(8,128)S(1)}, u32[]{:S(2)}, u32[]{:S(2)}) collective-permute-start(f32[8,640]{1,0:T(8,128)S(1)} %get-tuple-element.81), channel_id=1, source_target_pairs={{8,18},{9,23},{10,20},{11,17},{12,22},{13,19},{14,16},{15,21}} | collective-permute-start | bytes 61448 | tf_op jit(solution)/shard_map/ppermute | solution.py:589
  206.6 63.3 %collective-permute-start.39 = (bf16[64,640]{1,0:T(8,128)(2,1)S(1)}, bf16[64,640]{1,0:T(8,128)(2,1)S(1)}, u32[]{:S(2)}, u32[]{:S(2)}) collective-permute-start(bf16[64,640]{1,0:T(8,128)(2,1)S(1)} %get-tuple-element.80), channel_id=1, source_target_pairs={{8,17},{9,16},{10,19},{11,18},{12,21},{13,20},{14,23},{15,22}} | collective-permute-start | bytes 245768 | tf_op jit(solution)/shard_map/ppermute | solution.py:589
  207.9 60.0 %collective-permute-start.37 = (bf16[144,640]{1,0:T(8,128)(2,1)S(1)}, bf16[144,640]{1,0:T(8,128)(2,1)S(1)}, u32[]{:S(2)}, u32[]{:S(2)}) collective-permute-start(bf16[144,640]{1,0:T(8,128)(2,1)S(1)} %get-tuple-element.78), channel_id=1, source_target_pairs={{8,16},{9,17},{10,18},{11,19},{12,20},{13,21},{14,22},{15,23}} | collective-permute-start | bytes 552968 | tf_op jit(solution)/shard_map/ppermute | solution.py:589
  267.9 3.1 collective-permute-start.42
  289.2 14.3 %collective-permute-start.43 = (bf16[80,640]{1,0:T(8,128)(2,1)}, bf16[80,640]{1,0:T(8,128)(2,1)}, u32[]{:S(2)}, u32[]{:S(2)}) collective-permute-start(bf16[80,640]{1,0:T(8,128)(2,1)} %get-tuple-element.83), channel_id=1, source_target_pairs={{16,23},{17,18},{18,17},{19,20},{20,19},{21,22},{22,21},{23,16}} | collective-permute-start | bytes 307208 | tf_op jit(solution)/shard_map/ppermute | solution.py:589
  292.2 48.8 %collective-permute-start.51 = (bf16[768,320]{0,1:T(8,128)(2,1)}, bf16[768,320]{0,1:T(8,128)(2,1)}, u32[]{:S(2)}, u32[]{:S(2)}) collective-permute-start(bf16[768,320]{0,1:T(8,128)(2,1)} %copy.13), channel_id=1, source_target_pairs={{0,24},{1,25},{2,26},{3,27},{4,28},{5,29},{6,30},{7,31}} | collective-permute-start | bytes 1474568 | tf_op jit(solution)/shard_map/ppermute | solution.py:589
  293.7 10.6 %collective-permute-start.46 = (f32[8,640]{1,0:T(8,128)}, f32[8,640]{1,0:T(8,128)S(1)}, u32[]{:S(2)}, u32[]{:S(2)}) collective-permute-start(f32[8,640]{1,0:T(8,128)} %copy-done.21), channel_id=1, source_target_pairs={{16,20},{17,21},{18,22},{19,23},{20,16},{21,17},{22,18},{23,19}} | collective-permute-start | bytes 61448 | tf_op jit(solution)/shard_map/ppermute | solution.py:589
  297.2 7.1 %collective-permute-start.45 = (f32[8,640]{1,0:T(8,128)}, f32[8,640]{1,0:T(8,128)S(1)}, u32[]{:S(2)}, u32[]{:S(2)}) collective-permute-start(f32[8,640]{1,0:T(8,128)} %copy-done.21), channel_id=1, source_target_pairs={{16,18},{17,23},{18,20},{19,17},{20,22},{21,19},{22,16},{23,21}} | collective-permute-start | bytes 61448 | tf_op jit(solution)/shard_map/ppermute | solution.py:589
  300.9 6.1 %collective-permute-start.44 = (bf16[64,640]{1,0:T(8,128)(2,1)}, bf16[64,640]{1,0:T(8,128)(2,1)S(1)}, u32[]{:S(2)}, u32[]{:S(2)}) collective-permute-start(bf16[64,640]{1,0:T(8,128)(2,1)} %copy-done.22), channel_id=1, source_target_pairs={{16,17},{17,16},{18,19},{19,18},{20,21},{21,20},{22,23},{23,22}} | collective-permute-start | bytes 245768 | tf_op jit(solution)/shard_map/ppermute | solution.py:589
  305.1 3.1 collective-permute-start.47
  330.9 12.1 %collective-permute-start.48 = (bf16[144,640]{1,0:T(8,128)(2,1)}, bf16[144,640]{1,0:T(8,128)(2,1)}, u32[]{:S(2)}, u32[]{:S(2)}) collective-permute-start(bf16[144,640]{1,0:T(8,128)(2,1)} %get-tuple-element.86), channel_id=1, source_target_pairs={{16,24},{17,25},{18,26},{19,27},{20,28},{21,29},{22,30},{23,31}} | collective-permute-start | bytes 552968 | tf_op jit(solution)/shard_map/ppermute | solution.py:589
  332.9 10.1 %collective-permute-start.49 = (bf16[80,640]{1,0:T(8,128)(2,1)}, bf16[80,640]{1,0:T(8,128)(2,1)}, u32[]{:S(2)}, u32[]{:S(2)}) collective-permute-start(bf16[80,640]{1,0:T(8,128)(2,1)} %get-tuple-element.87), channel_id=1, source_target_pairs={{16,31},{17,26},{18,25},{19,28},{20,27},{21,30},{22,29},{23,24}} | collective-permute-start | bytes 307208 | tf_op jit(solution)/shard_map/ppermute | solution.py:589
  338.4 4.7 %collective-permute-start.50 = (bf16[64,640]{1,0:T(8,128)(2,1)}, bf16[64,640]{1,0:T(8,128)(2,1)}, u32[]{:S(2)}, u32[]{:S(2)}) collective-permute-start(bf16[64,640]{1,0:T(8,128)(2,1)} %get-tuple-element.88), channel_id=1, source_target_pairs={{16,25},{17,24},{18,27},{19,26},{20,29},{21,28},{22,31},{23,30}} | collective-permute-start | bytes 245768 | tf_op jit(solution)/shard_map/ppermute | solution.py:589
  359.0 2.0 collective-permute-start.55
  359.6 1.4 collective-permute-start.56
  360.3 0.7 collective-permute-start.54
  361.1 2.0 collective-permute-start.57
  361.8 1.4 collective-permute-start.53
  362.4 0.8 collective-permute-start.52
  375.5 2.7 collective-permute-start.58
  376.2 2.1 collective-permute-start.61
  376.9 1.4 collective-permute-start.60
  377.5 1.7 collective-permute-start.59
  378.4 0.9 collective-permute-start.62
  388.2 51.1 %collective-permute-start.63 = (bf16[8,16,320]{2,1,0:T(8,128)(2,1)S(1)}, bf16[8,16,320]{2,1,0:T(8,128)(2,1)S(1)}, u32[]{:S(2)}, u32[]{:S(2)}) collective-permute-start(bf16[8,16,320]{2,1,0:T(8,128)(2,1)S(1)} %get-tuple-element.100), channel_id=1, source_target_pairs={{24,0},{25,1},{26,2},{27,3},{28,4},{29,5},{30,6},{31,7}} | collective-permute-start | bytes 245768 | tf_op jit(solution)/shard_map/ppermute | solution.py:589
  425.3 14.0 %collective-permute-start.64 = (bf16[8,16,320]{2,1,0:T(8,128)(2,1)S(1)}, bf16[8,16,320]{2,1,0:T(8,128)(2,1)S(1)}, u32[]{:S(2)}, u32[]{:S(2)}) collective-permute-start(bf16[8,16,320]{2,1,0:T(8,128)(2,1)S(1)} %get-tuple-element.101), channel_id=1, source_target_pairs={{24,8},{25,9},{26,10},{27,11},{28,12},{29,13},{30,14},{31,15}} | collective-permute-start | bytes 245768 | tf_op jit(solution)/shard_map/ppermute | solution.py:589
  432.3 12.2 %collective-permute-start.65 = (bf16[8,16,320]{2,1,0:T(8,128)(2,1)S(1)}, bf16[8,16,320]{2,1,0:T(8,128)(2,1)S(1)}, u32[]{:S(2)}, u32[]{:S(2)}) collective-permute-start(bf16[8,16,320]{2,1,0:T(8,128)(2,1)S(1)} %get-tuple-element.102), channel_id=1, source_target_pairs={{24,16},{25,17},{26,18},{27,19},{28,20},{29,21},{30,22},{31,23}} | collective-permute-start | bytes 245768 | tf_op jit(solution)/shard_map/ppermute | solution.py:589
  (37 other events, 833.7 us)
where the time goes:
time: 454 us; the launch traced here: 446 us
  starting transfers between devices  160 us (35%)
  waiting for transfers between devices  130 us (29%)
  Pallas kernels  125 us (28%)
  local copies, waits for them, and re-layouts  20.9 us (5%)
  other arithmetic  7.97 us (2%)
    ppermute x50, starting transfers between devices, permute(): return lax.ppermute(value, ('section', 'space'), pairs)  107 us
    ppermute x50, waiting for transfers between devices, permute(): return lax.ppermute(value, ('section', 'space'), pairs)  66.9 us
    pallas_call x4, Pallas kernels, coarse_conv(): call(body, name, 1, 5 + extra, len(pieces), outs, scratch_of(weights, row...  64.2 us
    ppermute x16, waiting for transfers between devices, within(): return lax.ppermute(value, ('section', 'space'), pairs)  63.4 us
    ppermute x16, starting transfers between devices, within(): return lax.ppermute(value, ('section', 'space'), pairs)  53.1 us
    unnamed x72, local copies, waits for them, and re-layouts  17.5 us
    pallas_call x2, Pallas kernels, fine_conv(): call(body, name, 1, 5 + extra, n_pieces, outs, scratch_of(weights, image_...  15 us
    pallas_call x1, Pallas kernels, join_conv(): call(body, 'join', 1, 7, len(pieces), outs, scratch, flops)  12.3 us
  transfers between devices with their start and end apart: 66, of which 17 were waited for; matrix products, arithmetic and copies ran while one was open for 3% of the time, Pallas kernels for 13%

commit v1 on v0

--- a/solution.py
+++ b/solution.py
@@ -140,38 +140,37 @@
 
     def copies(self, flags, stack_refs, buffer, sems):
         made = []
+        lanes = self.shape.lanes
         for dy in range(3):
             mine = []
-            for block in range(self.blocks):
-                at = self.start + dy * self.blocks + block
-                for low, high, owners in self.bounds:
-                    if low <= at < high:
-                        for ref, owner in zip(stack_refs[low], owners, strict=True):
-                            for j in range(ref.shape[0]):
-                                mine.append(
-                                    pltpu.make_async_copy(
-                                        ref.at[j, at - low],
-                                        buffer.at[dy, block, owner(flags, j)],
-                                        sems.at[dy, len(mine)],
-                                    )
-                                )
+            begin = self.start + dy * self.blocks
+            for low, high, owners in self.bounds:
+                a, b = max(begin, low), min(begin + self.blocks, high)
+                if a >= b:
+                    continue
+                for ref, owner in zip(stack_refs[low], owners, strict=True):
+                    for j in range(ref.shape[0]):
+                        mine.append(
+                            pltpu.make_async_copy(
+                                ref.at[j, :, (a - low) * lanes : (b - low) * lanes],
+                                self.slot(buffer.at[dy], owner(flags, j), a - begin, b - begin),
+                                sems.at[dy, len(mine)],
+                            )
+                        )
             made.append(mine)
         return made
 
+    def slot(self, target, owner, first, last):
+        lanes = self.shape.lanes
+        if not self.split:
+            return target.at[owner, :, first * lanes : last * lanes]
+        half = self.shape.m // 2
+        shift = pl.multiple_of(owner // half * self.depth, lanes)
+        return target.at[owner % half, :, pl.ds(first * lanes + shift, (last - first) * lanes)]
+
     def product(self, left, buffer, dy):
-        shape = self.shape
-        rows = shape.m * shape.cols_of
-        total = None
-        for block in range(self.blocks):
-            right = buffer[dy, block].reshape(rows, shape.lanes)
-            for odd in range(2 if self.split else 1):
-                part = right[odd * self.c_out : (odd + 1) * self.c_out] if self.split else right
-                begin = (odd * self.blocks + block) * shape.lanes
-                made = lax.dot_general(
-                    left[:, begin : begin + shape.lanes], part, (((1,), (1,)), ((), ())), preferred_element_type=F32
-                )
-                total = made if total is None else total + made
-        return total
+        right = buffer[dy].reshape(self.c_out, self.width)
+        return lax.dot_general(left, right, (((1,), (1,)), ((), ())), preferred_element_type=F32)
 
     def put(self, image, row, place, tap, value, first=0, channels=None):
         shape = self.shape
@@ -222,18 +221,18 @@
 
 def scratch_of(weights, image_rows, out_rows, width, extra=()):
     return [
-        pltpu.VMEM((3, weights.blocks, weights.shape.m, weights.shape.cols_of, weights.shape.lanes), BF16),
+        pltpu.VMEM((3, weights.c_out // weights.shape.cols_of, weights.shape.cols_of, weights.width), BF16),
         pltpu.VMEM((image_rows, width, weights.width), BF16),
         pltpu.VMEM((out_rows * width, weights.c_out), F32),
-        pltpu.SemaphoreType.DMA((3, 8 * weights.blocks)),
+        pltpu.SemaphoreType.DMA((3, 16)),
     ] + list(extra)
 
 
-def call(body, name, n_smem, n_vmem, n_any, outs, scratch, flops, limit=24 * 1024 * 1024):
+def call(body, name, n_smem, n_vmem, n_any, outs, scratch, flops, limit=60 * 1024 * 1024):
     specs = (
         [pl.BlockSpec(memory_space=pltpu.SMEM)] * n_smem
         + [pl.BlockSpec(memory_space=pltpu.VMEM)] * n_vmem
-        + [pl.BlockSpec(memory_space=pl.ANY)] * n_any
+        + [pl.BlockSpec(memory_space=pltpu.HBM)] * n_any
     )
     return pl.pallas_call(
         body,
@@ -508,7 +507,9 @@
                 for ref, owner in zip(weights.stacks(piece_refs)[low], owners, strict=True):
                     for j in range(ref.shape[0]):
                         copy = pltpu.make_async_copy(
-                            ref.at[j, j_block - low], jbuf.at[owner(flags, j)], jsem.at[len(jcopies)]
+                            ref.at[j, :, (j_block - low) * shape.lanes : (j_block - low + 1) * shape.lanes],
+                            jbuf.at[owner(flags, j)],
+                            jsem.at[len(jcopies)],
                         )
                         copy.start()
                         jcopies.append(copy)
@@ -564,12 +565,13 @@
         for block in range(count):
             part = rows[block * shape.blk : (block + 1) * shape.blk, :]
             made = lax.dot_general(same, part, (((1,), (1,)), ((), ())), preferred_element_type=F32)
-            out_ref[block, :, 0 : shape.blk] = made.astype(BF16)
-            out_ref[block, :, shape.blk :] = jnp.zeros((columns, shape.lanes - shape.blk), BF16)
+            begin, end = block * shape.lanes, (block + 1) * shape.lanes
+            out_ref[:, begin : begin + shape.blk] = made.astype(BF16)
+            out_ref[:, begin + shape.blk : end] = jnp.zeros((columns, shape.lanes - shape.blk), BF16)
 
     scratch = [pltpu.VMEM((count * shape.blk, columns), BF16), pltpu.SemaphoreType.DMA(())]
-    outs = [((count, columns, shape.lanes), BF16)]
-    return call(body, f"pack{low}", 0, 0, 1, outs, scratch, 1000, 16 * 1024 * 1024)(pack)[0]
+    outs = [((columns, count * shape.lanes), BF16)]
+    return call(body, f"pack{low}", 0, 0, 1, outs, scratch, 1000)(pack)[0]
 
 
 def shards(n, n_section, features, section_packs):
@@ -581,7 +583,7 @@
     flags = jnp.stack([w % 2, (w == 0).astype(jnp.int32), (w == n - 1).astype(jnp.int32), section_id, w]).astype(jnp.int32)
 
     total = pack.shape[0] // shape.blk
-    cuts = [0, 9 * q_rows // shape.blk, 18 * q_rows // shape.blk, 36 * q_rows // shape.blk, total]
+    cuts = [0, 9 * q_rows // shape.blk, 36 * q_rows // shape.blk, total]
     bounds = list(zip(cuts[:-1], cuts[1:], strict=True))
 
     def permute(value, source, target, move):
@@ -646,25 +648,30 @@
     def owner_far(flags, j):
         return ((flags[4] // 2) ^ j) * 2 + 1 - flags[0]
 
-    pieces = []
-    previous = None
-    for number, (low, high) in enumerate(bounds):
+    def after(value, *deps):
+        return lax.optimization_barrier((value,) + deps)[0]
+
+    pieces = {}
+
+    def send(number, *deps):
+        low, high = bounds[number]
         if n == 8:
-            planes = range(n_section) if number < 3 else range(1, n_section)
-            own = pack_blocks(shape, pack, low, high)
-            if previous is not None:
-                own, _ = lax.optimization_barrier((own, previous))
-            got = [within(own, planes, lambda i, k=k: i ^ (2 * k)) for k in range(1, 4)]
-            previous = got
-            near = jnp.stack([own] + got)
-            far = within(near, planes, partner)
-            pieces.append(([near, far], [owner_near, owner_far]))
+            planes = range(n_section) if number < 2 else range(1, n_section)
+            own = after(pack_blocks(shape, pack, low, high), *deps)
+            return [own] + [within(own, planes, lambda i, k=k: i ^ (2 * k)) for k in range(1, 4)]
+        got = lax.all_gather(pack[low * shape.blk : high * shape.blk], "space")
+        got = got.reshape(shape.m, n // shape.m, high - low, shape.blk, -1).transpose(0, 1, 4, 2, 3)
+        got = got.reshape(shape.m, shape.cols_of, high - low, shape.blk)
+        got = jnp.pad(got, ((0, 0), (0, 0), (0, 0), (0, shape.lanes - shape.blk)))
+        return [got.reshape(shape.m, shape.cols_of, -1)]
+
+    def finish(number, got, *deps):
+        if n == 8:
+            near = after(jnp.stack(got), *deps)
+            far = within(near, range(n_section) if number < 2 else range(1, n_section), partner)
+            pieces[number] = ([near, far], [owner_near, owner_far])
         else:
-            got = lax.all_gather(pack[low * shape.blk : high * shape.blk], "space")
-            got = got.reshape(shape.m, n // shape.m, high - low, shape.blk, -1).transpose(0, 2, 1, 4, 3)
-            got = got.reshape(shape.m, high - low, shape.cols_of, shape.blk)
-            got = jnp.pad(got, ((0, 0), (0, 0), (0, 0), (0, shape.lanes - shape.blk)))
-            pieces.append(([got], [lambda flags, j: j]))
+            pieces[number] = (got, [lambda flags, j: j])
 
     def weights(start, c_in, c_out, parts):
         first = start // shape.blk
@@ -675,9 +682,14 @@
 
     narrow, wide = shape.narrow, shape.wide
     x = features[0].reshape(shape.rows, shape.half, 2, narrow).transpose(0, 2, 1, 3).reshape(-1, narrow)
-    first = exchange(prepare(shape, flags, x, 1), 0, 0)
+    sent = send(0)
+    first = exchange(prepare(shape, flags, after(x, sent[0]), 1), 0, 0)
+    finish(0, sent)
+    sent = send(1, sent, first)
     hidden = fine_conv(shape, flags, *weights(0, narrow, narrow, (narrow,)), first, 1, 0, 2, name="c00")
     second = exchange(hidden, 0, 0)
+    finish(1, sent, second)
+    sent = send(2, sent, pieces[1][0])
     (skip,) = fine_conv(
         shape, flags, *weights(9 * q_rows, narrow, narrow, (narrow,)), second, 2, 1, 0, residual=first[:3], name="c01"
     )
@@ -688,6 +700,8 @@
             skip, got = lax.optimization_barrier((skip, got))
             skip = permute(skip, 0, 3, lambda i: i)
         hidden = coarse_conv(shape, flags, *weights(0, wide, wide, (wide,)), got, 1, name=f"c{section}0")
+        if section == 1:
+            finish(2, sent, hidden[3])
         then = exchange(hidden, section, section)
         coarse = coarse_conv(
             shape, flags, *weights(36 * q_rows, wide, wide, (wide,)), then, 1, residual=got[0], name=f"c{section}1"

time: 454 us -> 388 us (0.85)
  Pallas kernels: 125 us -> 90.5 us
  waiting for transfers between devices: 130 us -> 104 us
    pallas_call x4, Pallas kernels: 64.2 us -> 31.8 us  [coarse_conv(): call(body, name, 1, 5 + extra, len(pieces), outs, scratch_of(weights, row...]
    ppermute x50, waiting for transfers between devices: 66.9 us -> 36.7 us  [permute(): return lax.ppermute(value, ('section', 'space'), pairs)]
    unnamed x72 -> x108, local copies, waits for them, and re-layouts: 17.5 us -> 13.9 us
    ppermute x16 -> x12, waiting for transfers between devices: 63.4 us -> 66.9 us  [within(): return lax.ppermute(value, ('section', 'space'), pairs)]
    ppermute x16 -> x12, starting transfers between devices: 53.1 us -> 49.9 us  [within(): return lax.ppermute(value, ('section', 'space'), pairs)]
  transfers between devices with their start and end apart: 66 -> 62, of which waited for: 17 -> 15; matrix products, arithmetic and copies ran while one was open for 3% -> 2% of each run, Pallas kernels for 13% -> 6%
where the time goes in v1:
time: 388 us; the launch traced here: 381 us
  starting transfers between devices  158 us (41%)
  waiting for transfers between devices  104 us (27%)
  Pallas kernels  90.5 us (23%)
  local copies, waits for them, and re-layouts  17.6 us (5%)
  other arithmetic  9.98 us (3%)
    ppermute x50, starting transfers between devices, permute(): return lax.ppermute(value, ('section', 'space'), pairs)  108 us
    ppermute x12, waiting for transfers between devices, within(): return lax.ppermute(value, ('section', 'space'), pairs)  66.9 us
    ppermute x12, starting transfers between devices, within(): return lax.ppermute(value, ('section', 'space'), pairs)  49.9 us
    ppermute x50, waiting for transfers between devices, permute(): return lax.ppermute(value, ('section', 'space'), pairs)  36.7 us
    pallas_call x4, Pallas kernels, coarse_conv(): call(body, name, 1, 5 + extra, len(pieces), outs, scratch_of(weights, row...  31.8 us
    pallas_call x2, Pallas kernels, fine_conv(): call(body, name, 1, 5 + extra, n_pieces, outs, scratch_of(weights, image_...  15.6 us
    unnamed x108, local copies, waits for them, and re-layouts  13.9 us
    pallas_call x1, Pallas kernels, join_conv(): call(body, 'join', 1, 7, len(pieces), outs, scratch, flops)  10 us
  transfers between devices with their start and end apart: 62, of which 15 were waited for; matrix products, arithmetic and copies ran while one was open for 2% of the time, Pallas kernels for 6%

profile of v1, /device:TPU:16, one launch (start us, length us, event | category | flops | bytes accessed | tf_op | source)
XLA Modules:
  0.0 381.4 jit_solution(2766470333522980897)
XLA Ops:
  0.0 4.4 %copy.12 = bf16[1,11520,80]{2,1,0:T(8,128)(2,1)} copy(bf16[1,11520,80]{1,2,0:T(8,128)(2,1)} %param.3) | data formatting | bytes 3686400 | tf_op args[1]
  4.4 2.0 pack0.1
  6.4 2.5 collective-permute-start.7
  9.9 6.5 %collective-permute-done.7 = bf16[80,1536]{1,0:T(8,128)(2,1)S(1)} collective-permute-done((bf16[80,1536]{1,0:T(8,128)(2,1)}, bf16[80,1536]{1,0:T(8,128)(2,1)S(1)}, u32[]{:S(2)}, u32[]{:S(2)}) %collective-permute-start.7) | collective-permute-done | bytes 245792 | tf_op jit(solution)/shard_map/ppermute | solution.py:643
  16.4 4.1 %collective-permute-done.6 = bf16[80,1536]{1,0:T(8,128)(2,1)S(1)} collective-permute-done((bf16[80,1536]{1,0:T(8,128)(2,1)}, bf16[80,1536]{1,0:T(8,128)(2,1)S(1)}, u32[]{:S(2)}, u32[]{:S(2)}) %collective-permute-start.6) | collective-permute-done | bytes 245792 | tf_op jit(solution)/shard_map/ppermute | solution.py:643
  20.6 1.1 pad_maximum_fusion.2.rest_0_
  22.1 0.8 copy.11
  23.5 2.1 prepare.1
  30.9 7.2 %c00.1 = (bf16[528,320]{1,0:T(8,128)(2,1)}, bf16[272,320]{1,0:T(8,128)(2,1)}, bf16[256,320]{1,0:T(8,128)(2,1)}, f32[8,320]{1,0:T(8,128)}) custom-call(s32[5]{0:T(128)} %stack.76.flags, bf16[528,320]{1,0:T(8,128)(2,1)} %get-tuple-element.57.block.rest_0_, bf16[144,320]{1,0:T(8,128)(2,1)} %copy-done.19, bf16[128,320]{1,0:T(8,128)(2,1)} %copy-done.23, ...), custom_call_target="tpu_custom_call" | custom-call | flops 943718400 | bytes 4000000 | tf_op jit(solution)/shard_map/c00/pallas_call | solution.py:315
  38.1 0.8 collective-permute-start.9
  38.9 2.7 pack3.1
  41.7 1.7 collective-permute-start.16
  43.4 1.3 collective-permute-start.15
  47.4 0.8 collective-permute-start.13
  48.2 14.0 %collective-permute-done.16 = bf16[80,4608]{1,0:T(8,128)(2,1)S(1)} collective-permute-done((bf16[80,4608]{1,0:T(8,128)(2,1)}, bf16[80,4608]{1,0:T(8,128)(2,1)S(1)}, u32[]{:S(2)}, u32[]{:S(2)}) %collective-permute-start.16) | collective-permute-done | bytes 737312 | tf_op jit(solution)/shard_map/ppermute | solution.py:643
  62.2 15.3 %collective-permute-done.15 = bf16[80,4608]{1,0:T(8,128)(2,1)S(1)} collective-permute-done((bf16[80,4608]{1,0:T(8,128)(2,1)}, bf16[80,4608]{1,0:T(8,128)(2,1)S(1)}, u32[]{:S(2)}, u32[]{:S(2)}) %collective-permute-start.15) | collective-permute-done | bytes 737312 | tf_op jit(solution)/shard_map/ppermute | solution.py:643
  77.5 1.4 pad_maximum_fusion.1.rest_3_.rest_0_.rest_2_
  79.1 5.5 %collective-permute-done.17.rest_4_.rest_1_.rest_3_ = bf16[4,80,4608]{2,1,0:T(8,128)(2,1)} collective-permute-done((bf16[4,80,4608]{2,1,0:T(8,128)(2,1)S(1)}, bf16[4,80,4608]{2,1,0:T(8,128)(2,1)}, u32[]{:S(2)}, u32[]{:S(2)}) %collective-permute-start.17) | collective-permute-done | bytes 2949152 | tf_op jit(solution)/shard_map/ppermute | solution.py:643
  84.6 8.4 %c01.1.skip_ref = bf16[768,320]{1,0:T(8,128)(2,1)} custom-call(s32[5]{0:T(128)} %stack.76.flags, bf16[528,320]{1,0:T(8,128)(2,1)} %get-tuple-element.61.block, bf16[272,320]{1,0:T(8,128)(2,1)} %copy-done.12, bf16[256,320]{1,0:T(8,128)(2,1)} %copy-done.13, f32[8,320]{1,0:T(8,128)} %copy-done.35, f32[8,320]{1,0:T(8,128)} %copy-done.42, ...), custom_call_target="tpu_custom_call" | custom-call | flops 1415577600 | bytes 4000000 | tf_op jit(solution)/shard_map/c01/pallas_call | solution.py:315
  93.0 5.5 %down.1 = (bf16[144,640]{1,0:T(8,128)(2,1)}, bf16[80,640]{1,0:T(8,128)(2,1)}, bf16[64,640]{1,0:T(8,128)(2,1)}, f32[8,640]{1,0:T(8,128)}) custom-call(s32[5]{0:T(128)} %stack.76.flags, bf16[768,320]{1,0:T(8,128)(2,1)} %c01.1.skip_ref, bf16[4,80,4608]{2,1,0:T(8,128)(2,1)} %copy-done, bf16[4,80,4608]{2,1,0:T(8,128)(2,1)} %collective-permute-done.17.rest_4_.rest_1_.rest_3_), custom_call_target="tpu_custom_call" | custom-call | flops 471859200 | bytes 4000000 | tf_op jit(solution)/shard_map/down/pallas_call | solution.py:357
  99.3 3.1 pack12.1
  102.4 23.4 %collective-permute-start.31 = (bf16[80,6144]{1,0:T(8,128)(2,1)}, bf16[80,6144]{1,0:T(8,128)(2,1)S(1)}, u32[]{:S(2)}, u32[]{:S(2)}) collective-permute-start(bf16[80,6144]{1,0:T(8,128)(2,1)} %pack12.1), channel_id=1, source_target_pairs={{8,14},{9,15},{10,12},{11,13},{12,10},{13,11},{14,8},{15,9},{16,22... | collective-permute-start | bytes 2949128 | tf_op jit(solution)/shard_map/ppermute | solution.py:643
  125.8 7.0 %collective-permute-start.30 = (bf16[80,6144]{1,0:T(8,128)(2,1)}, bf16[80,6144]{1,0:T(8,128)(2,1)S(1)}, u32[]{:S(2)}, u32[]{:S(2)}) collective-permute-start(bf16[80,6144]{1,0:T(8,128)(2,1)} %pack12.1), channel_id=1, source_target_pairs={{8,12},{9,13},{10,14},{11,15},{12,8},{13,9},{14,10},{15,11},{16,20... | collective-permute-start | bytes 2949128 | tf_op jit(solution)/shard_map/ppermute | solution.py:643
  132.8 7.0 %collective-permute-start.29 = (bf16[80,6144]{1,0:T(8,128)(2,1)}, bf16[80,6144]{1,0:T(8,128)(2,1)S(1)}, u32[]{:S(2)}, u32[]{:S(2)}) collective-permute-start(bf16[80,6144]{1,0:T(8,128)(2,1)} %pack12.1), channel_id=1, source_target_pairs={{8,10},{9,11},{10,8},{11,9},{12,14},{13,15},{14,12},{15,13},{16,18... | collective-permute-start | bytes 2949128 | tf_op jit(solution)/shard_map/ppermute | solution.py:643
  144.7 7.9 %c10.1 = (bf16[144,640]{1,0:T(8,128)(2,1)}, bf16[80,640]{1,0:T(8,128)(2,1)}, bf16[64,640]{1,0:T(8,128)(2,1)}, f32[8,640]{1,0:T(8,128)}) custom-call(s32[5]{0:T(128)} %stack.76.flags, bf16[144,640]{1,0:T(8,128)(2,1)} %copy-done.9, bf16[80,640]{1,0:T(8,128)(2,1)} %copy-done.15, bf16[64,640]{1,0:T(8,128)(2,1)} %copy-done.29, f32[8,640]{1,0:T(8,128)} %copy-done.32, ...), custom_call_target="tpu_custom_call" | custom-call | flops 943718400 | bytes 4000000 | tf_op jit(solution)/shard_map/c10/pallas_call | solution.py:393
  152.7 18.8 %collective-permute-done.30 = bf16[80,6144]{1,0:T(8,128)(2,1)S(1)} collective-permute-done((bf16[80,6144]{1,0:T(8,128)(2,1)}, bf16[80,6144]{1,0:T(8,128)(2,1)S(1)}, u32[]{:S(2)}, u32[]{:S(2)}) %collective-permute-start.30) | collective-permute-done | bytes 983072 | tf_op jit(solution)/shard_map/ppermute | solution.py:643
  171.5 0.9 copy-done.7
  172.8 2.4 pad_maximum_fusion.rest_1_.rest_0_
  175.2 5.2 %collective-permute-start.32 = (bf16[4,80,6144]{2,1,0:T(8,128)(2,1)S(1)}, bf16[4,80,6144]{2,1,0:T(8,128)(2,1)S(1)}, u32[]{:S(2)}, u32[]{:S(2)}) collective-permute-start(bf16[4,80,6144]{2,1,0:T(8,128)(2,1)S(1)} %pad_maximum_fusion.rest_1_.rest_0_), channel_id=1, source_target_pairs={{8,9},{9,8},{10,11},{11,10},{12,13},{13,12},{14,15},{15,14},{16,17... | collective-permute-start | bytes 11796488 | tf_op jit(solution)/shard_map/ppermute | solution.py:643
  183.3 0.9 collective-permute-start.28
  184.2 2.6 collective-permute-done.32.rest_2_.rest_1_
  186.8 1.9 copy-done.2
  188.7 8.0 %c11.1 = (bf16[144,640]{1,0:T(8,128)(2,1)}, bf16[80,640]{1,0:T(8,128)(2,1)}, bf16[64,640]{1,0:T(8,128)(2,1)}, f32[8,640]{1,0:T(8,128)}) custom-call(s32[5]{0:T(128)} %stack.76.flags, bf16[144,640]{1,0:T(8,128)(2,1)} %get-tuple-element.76.block, bf16[80,640]{1,0:T(8,128)(2,1)} %copy-done.18, bf16[64,640]{1,0:T(8,128)(2,1)} %copy-done.27, ...), custom_call_target="tpu_custom_call" | custom-call | flops 943718400 | bytes 4000000 | tf_op jit(solution)/shard_map/c11/pallas_call | solution.py:393
  196.7 1.3 collective-permute-start.34
  198.0 1.3 collective-permute-start.37
  199.3 1.3 collective-permute-start.36
  200.6 1.3 collective-permute-start.35
  201.9 1.3 collective-permute-start.33
  203.2 8.9 %collective-permute-done.34.outer = bf16[80,640]{1,0:T(8,128)(2,1)S(1)} collective-permute-done((bf16[80,640]{1,0:T(8,128)(2,1)}, bf16[80,640]{1,0:T(8,128)(2,1)S(1)}, u32[]{:S(2)}, u32[]{:S(2)}) %collective-permute-start.34) | collective-permute-done | bytes 102432 | tf_op jit(solution)/shard_map/ppermute | solution.py:591
  212.1 18.2 %collective-permute-done.33.block.rest_0_ = bf16[144,640]{1,0:T(8,128)(2,1)S(1)} collective-permute-done((bf16[144,640]{1,0:T(8,128)(2,1)}, bf16[144,640]{1,0:T(8,128)(2,1)S(1)}, u32[]{:S(2)}, u32[]{:S(2)}) %collective-permute-start.33) | collective-permute-done | bytes 184352 | tf_op jit(solution)/shard_map/ppermute | solution.py:591
  230.5 2.1 collective-permute-start.38
  232.6 1.1 collective-permute-done.38.sb
  234.3 8.0 %c20.1 = (bf16[144,640]{1,0:T(8,128)(2,1)}, bf16[80,640]{1,0:T(8,128)(2,1)}, bf16[64,640]{1,0:T(8,128)(2,1)}, f32[8,640]{1,0:T(8,128)}) custom-call(s32[5]{0:T(128)} %stack.76.flags, bf16[144,640]{1,0:T(8,128)(2,1)} %copy-done.10, bf16[80,640]{1,0:T(8,128)(2,1)} %copy-done.16, bf16[64,640]{1,0:T(8,128)(2,1)} %copy-done.26, f32[8,640]{1,0:T(8,128)} %copy-done.33, ...), custom_call_target="tpu_custom_call" | custom-call | flops 943718400 | bytes 4000000 | tf_op jit(solution)/shard_map/c20/pallas_call | solution.py:393
  242.3 1.9 collective-permute-start.39
  245.2 3.7 collective-permute-start.42
  248.9 3.3 collective-permute-start.41
  252.2 2.6 collective-permute-start.40
  256.5 1.9 collective-permute-start.43
  258.4 1.1 collective-permute-done.43.sb
  260.2 8.0 %c21.1 = (bf16[144,640]{1,0:T(8,128)(2,1)}, bf16[80,640]{1,0:T(8,128)(2,1)}, bf16[64,640]{1,0:T(8,128)(2,1)}, f32[8,640]{1,0:T(8,128)}) custom-call(s32[5]{0:T(128)} %stack.76.flags, bf16[144,640]{1,0:T(8,128)(2,1)} %get-tuple-element.86.block, bf16[80,640]{1,0:T(8,128)(2,1)} %copy-done.17, bf16[64,640]{1,0:T(8,128)(2,1)} %copy-done.28, ...), custom_call_target="tpu_custom_call" | custom-call | flops 943718400 | bytes 4000000 | tf_op jit(solution)/shard_map/c21/pallas_call | solution.py:393
  268.1 1.3 collective-permute-start.44
  269.4 4.8 %collective-permute-start.45 = (bf16[80,640]{1,0:T(8,128)(2,1)}, bf16[80,640]{1,0:T(8,128)(2,1)S(1)}, u32[]{:S(2)}, u32[]{:S(2)}) collective-permute-start(bf16[80,640]{1,0:T(8,128)(2,1)} %get-tuple-element.91), channel_id=1, source_target_pairs={{16,31},{17,26},{18,25},{19,28},{20,27},{21,30},{22,29},{23,24}} | collective-permute-start | bytes 307208 | tf_op jit(solution)/shard_map/ppermute | solution.py:591
  274.2 6.8 %collective-permute-start.46 = (bf16[64,640]{1,0:T(8,128)(2,1)}, bf16[64,640]{1,0:T(8,128)(2,1)S(1)}, u32[]{:S(2)}, u32[]{:S(2)}) collective-permute-start(bf16[64,640]{1,0:T(8,128)(2,1)} %get-tuple-element.92), channel_id=1, source_target_pairs={{16,25},{17,24},{18,27},{19,26},{20,29},{21,28},{22,31},{23,30}} | collective-permute-start | bytes 245768 | tf_op jit(solution)/shard_map/ppermute | solution.py:591
  281.0 1.1 copy.14.skip_ref
  282.1 1.0 collective-permute-done.46.inner
  284.5 9.2 %up.1 = (bf16[528,320]{1,0:T(8,128)(2,1)}, bf16[144,320]{1,0:T(8,128)(2,1)}, bf16[128,320]{1,0:T(8,128)(2,1)}, f32[8,320]{1,0:T(8,128)}, f32[8,320]{1,0:T(8,128)}) custom-call(s32[5]{0:T(128)} %stack.76.flags, bf16[144,640]{1,0:T(8,128)(2,1)} %copy-done.14, bf16[80,640]{1,0:T(8,128)(2,1)} %copy-done.22, bf16[64,640]{1,0:T(8,128)(2,1)} %copy-done.34, ...), custom_call_target="tpu_custom_call" | custom-call | flops 1887436800 | bytes 4000000 | tf_op jit(solution)/shard_map/up/pallas_call | solution.py:432
  296.5 0.8 add_add_fusion.1
  300.7 10.0 %join.1 = (bf16[528,320]{1,0:T(8,128)(2,1)}, bf16[144,320]{1,0:T(8,128)(2,1)}, bf16[128,320]{1,0:T(8,128)(2,1)}, f32[8,320]{1,0:T(8,128)}) custom-call(s32[5]{0:T(128)} %stack.76.flags, bf16[528,320]{1,0:T(8,128)(2,1)} %get-tuple-element.94.block.u_ref, bf16[144,320]{1,0:T(8,128)(2,1)} %copy-done.21, bf16[128,320]{1,0:T(8,128)(2,1)} %copy-done.25, ...), custom_call_target="tpu_custom_call" | custom-call | flops 1887436800 | bytes 4000000 | tf_op jit(solution)/shard_map/join/pallas_call | solution.py:473
  314.3 0.8 collective-permute-start.58
  315.8 8.4 %last.1 = (bf16[8,16,320]{2,1,0:T(8,128)(2,1)}, bf16[8,16,320]{2,1,0:T(8,128)(2,1)}, bf16[8,16,320]{2,1,0:T(8,128)(2,1)}, bf16[8,16,320]{2,1,0:T(8,128)(2,1)}) custom-call(s32[5]{0:T(128)} %stack.76.flags, bf16[528,320]{1,0:T(8,128)(2,1)} %get-tuple-element.99.block, bf16[144,320]{1,0:T(8,128)(2,1)} %copy-done.20, bf16[128,320]{1,0:T(8,128)(2,1)} %copy-done.24, ...), custom_call_target="tpu_custom_call" | custom-call | flops 1153433600 | bytes 4000000 | tf_op jit(solution)/shard_map/last/pallas_call | solution.py:552
  324.2 36.7 %collective-permute-start.59 = (bf16[8,16,320]{2,1,0:T(8,128)(2,1)}, bf16[8,16,320]{2,1,0:T(8,128)(2,1)S(1)}, u32[]{:S(2)}, u32[]{:S(2)}) collective-permute-start(bf16[8,16,320]{2,1,0:T(8,128)(2,1)} %get-tuple-element.104), channel_id=1, source_target_pairs={{24,0},{25,1},{26,2},{27,3},{28,4},{29,5},{30,6},{31,7}} | collective-permute-start | bytes 245768 | tf_op jit(solution)/shard_map/ppermute | solution.py:591
  360.9 7.0 %collective-permute-start.60 = (bf16[8,16,320]{2,1,0:T(8,128)(2,1)}, bf16[8,16,320]{2,1,0:T(8,128)(2,1)S(1)}, u32[]{:S(2)}, u32[]{:S(2)}) collective-permute-start(bf16[8,16,320]{2,1,0:T(8,128)(2,1)} %get-tuple-element.105), channel_id=1, source_target_pairs={{24,8},{25,9},{26,10},{27,11},{28,12},{29,13},{30,14},{31,15}} | collective-permute-start | bytes 245768 | tf_op jit(solution)/shard_map/ppermute | solution.py:591
  367.9 7.0 %collective-permute-start.61 = (bf16[8,16,320]{2,1,0:T(8,128)(2,1)}, bf16[8,16,320]{2,1,0:T(8,128)(2,1)S(1)}, u32[]{:S(2)}, u32[]{:S(2)}) collective-permute-start(bf16[8,16,320]{2,1,0:T(8,128)(2,1)} %get-tuple-element.106), channel_id=1, source_target_pairs={{24,16},{25,17},{26,18},{27,19},{28,20},{29,21},{30,22},{31,23}} | collective-permute-start | bytes 245768 | tf_op jit(solution)/shard_map/ppermute | solution.py:591
  374.9 5.4 %collective-permute-done.61 = bf16[8,16,320]{2,1,0:T(8,128)(2,1)S(1)} collective-permute-done((bf16[8,16,320]{2,1,0:T(8,128)(2,1)}, bf16[8,16,320]{2,1,0:T(8,128)(2,1)S(1)}, u32[]{:S(2)}, u32[]{:S(2)}) %collective-permute-start.61) | collective-permute-done | bytes 81952 | tf_op jit(solution)/shard_map/ppermute | solution.py:591
  (222 shorter events, 34.9 us)
Async XLA Ops:
  6.4 10.0 %collective-permute-start.7 = (bf16[80,1536]{1,0:T(8,128)(2,1)}, bf16[80,1536]{1,0:T(8,128)(2,1)S(1)}, u32[]{:S(2)}, u32[]{:S(2)}) collective-permute-start(bf16[80,1536]{1,0:T(8,128)(2,1)} %pack0.1), channel_id=1, source_target_pairs={{0,6},{1,7},{2,4},{3,5},{4,2},{5,3},{6,0},{7,1},{8,14},{9,15},{10,... | collective-permute-start | bytes 737288 | tf_op jit(solution)/shard_map/ppermute | solution.py:643
  8.9 11.6 %collective-permute-start.6 = (bf16[80,1536]{1,0:T(8,128)(2,1)}, bf16[80,1536]{1,0:T(8,128)(2,1)S(1)}, u32[]{:S(2)}, u32[]{:S(2)}) collective-permute-start(bf16[80,1536]{1,0:T(8,128)(2,1)} %pack0.1), channel_id=1, source_target_pairs={{0,4},{1,5},{2,6},{3,7},{4,0},{5,1},{6,2},{7,3},{8,12},{9,13},{10,... | collective-permute-start | bytes 737288 | tf_op jit(solution)/shard_map/ppermute | solution.py:643
  9.4 11.2 %collective-permute-start.5 = (bf16[80,1536]{1,0:T(8,128)(2,1)}, bf16[80,1536]{1,0:T(8,128)(2,1)S(1)}, u32[]{:S(2)}, u32[]{:S(2)}) collective-permute-start(bf16[80,1536]{1,0:T(8,128)(2,1)} %pack0.1), channel_id=1, source_target_pairs={{0,2},{1,3},{2,0},{3,1},{4,6},{5,7},{6,4},{7,5},{8,10},{9,11},{10,... | collective-permute-start | bytes 737288 | tf_op jit(solution)/shard_map/ppermute | solution.py:643
  21.7 8.2 %collective-permute-start.8 = (bf16[4,80,1536]{2,1,0:T(8,128)(2,1)S(1)}, bf16[4,80,1536]{2,1,0:T(8,128)(2,1)S(1)}, u32[]{:S(2)}, u32[]{:S(2)}) collective-permute-start(bf16[4,80,1536]{2,1,0:T(8,128)(2,1)S(1)} %pad_maximum_fusion.2.rest_0_), channel_id=1, source_target_pairs={{0,1},{1,0},{2,3},{3,2},{4,5},{5,4},{6,7},{7,6},{8,9},{9,8},{10,11... | collective-permute-start | bytes 2949128 | tf_op jit(solution)/shard_map/ppermute | solution.py:643
  25.6 2.8 collective-permute-start
  26.3 2.1 collective-permute-start.3
  26.9 1.5 collective-permute-start.2
  27.6 2.3 collective-permute-start.1
  29.2 0.7 collective-permute-start.4
  38.1 7.8 %collective-permute-start.9 = (bf16[272,320]{1,0:T(8,128)(2,1)}, bf16[272,320]{1,0:T(8,128)(2,1)S(1)}, u32[]{:S(2)}, u32[]{:S(2)}) collective-permute-start(bf16[272,320]{1,0:T(8,128)(2,1)} %get-tuple-element.62), channel_id=1, source_target_pairs={{0,7},{1,2},{2,1},{3,4},{4,3},{5,6},{6,5},{7,0}} | collective-permute-start | bytes 522248 | tf_op jit(solution)/shard_map/ppermute | solution.py:591
  41.7 20.6 %collective-permute-start.16 = (bf16[80,4608]{1,0:T(8,128)(2,1)}, bf16[80,4608]{1,0:T(8,128)(2,1)S(1)}, u32[]{:S(2)}, u32[]{:S(2)}) collective-permute-start(bf16[80,4608]{1,0:T(8,128)(2,1)} %pack3.1), channel_id=1, source_target_pairs={{0,6},{1,7},{2,4},{3,5},{4,2},{5,3},{6,0},{7,1},{8,14},{9,15},{10,... | collective-permute-start | bytes 2211848 | tf_op jit(solution)/shard_map/ppermute | solution.py:643
  43.4 34.1 %collective-permute-start.15 = (bf16[80,4608]{1,0:T(8,128)(2,1)}, bf16[80,4608]{1,0:T(8,128)(2,1)S(1)}, u32[]{:S(2)}, u32[]{:S(2)}) collective-permute-start(bf16[80,4608]{1,0:T(8,128)(2,1)} %pack3.1), channel_id=1, source_target_pairs={{0,4},{1,5},{2,6},{3,7},{4,0},{5,1},{6,2},{7,3},{8,12},{9,13},{10,... | collective-permute-start | bytes 2211848 | tf_op jit(solution)/shard_map/ppermute | solution.py:643
  44.7 32.8 %collective-permute-start.14 = (bf16[80,4608]{1,0:T(8,128)(2,1)}, bf16[80,4608]{1,0:T(8,128)(2,1)S(1)}, u32[]{:S(2)}, u32[]{:S(2)}) collective-permute-start(bf16[80,4608]{1,0:T(8,128)(2,1)} %pack3.1), channel_id=1, source_target_pairs={{0,2},{1,3},{2,0},{3,1},{4,6},{5,7},{6,4},{7,5},{8,10},{9,11},{10,... | collective-permute-start | bytes 2211848 | tf_op jit(solution)/shard_map/ppermute | solution.py:643
  45.2 1.4 collective-permute-start.12
  45.9 1.4 collective-permute-start.11
  46.6 32.3 %collective-permute-start.10 = (bf16[256,320]{1,0:T(8,128)(2,1)S(1)}, bf16[256,320]{1,0:T(8,128)(2,1)S(1)}, u32[]{:S(2)}, u32[]{:S(2)}) collective-permute-start(bf16[256,320]{1,0:T(8,128)(2,1)S(1)} %copy-done.46), channel_id=1, source_target_pairs={{0,1},{1,0},{2,3},{3,2},{4,5},{5,4},{6,7},{7,6}} | collective-permute-start | bytes 491528 | tf_op jit(solution)/shard_map/ppermute | solution.py:591
  47.4 31.6 %collective-permute-start.13 = (f32[8,320]{1,0:T(8,128)S(1)}, f32[8,320]{1,0:T(8,128)S(1)}, u32[]{:S(2)}, u32[]{:S(2)}) collective-permute-start(f32[8,320]{1,0:T(8,128)S(1)} %fusion.11.sa), channel_id=1, source_target_pairs={{0,1},{1,0},{2,3},{3,2},{4,5},{5,4},{6,7},{7,6}} | collective-permute-start | bytes 30728 | tf_op jit(solution)/shard_map/ppermute | solution.py:591
  79.0 5.6 %collective-permute-start.17 = (bf16[4,80,4608]{2,1,0:T(8,128)(2,1)S(1)}, bf16[4,80,4608]{2,1,0:T(8,128)(2,1)}, u32[]{:S(2)}, u32[]{:S(2)}) collective-permute-start(bf16[4,80,4608]{2,1,0:T(8,128)(2,1)S(1)} %pad_maximum_fusion.1.rest_3_.rest_0_.rest_2_), channel_id=1, source_target_pairs={{0,1},{1,0},{2,3},{3,2},{4,5},{5,4},{6,7},{7,6},{8,9},{9,8},{10,11... | collective-permute-start | bytes 8847368 | tf_op jit(solution)/shard_map/ppermute | solution.py:643
  98.5 42.1 %copy-start.47 = (bf16[144,640]{1,0:T(8,128)(2,1)S(1)}, bf16[144,640]{1,0:T(8,128)(2,1)}, u32[]{:S(2)}) copy-start(bf16[144,640]{1,0:T(8,128)(2,1)} %get-tuple-element.67) | copy-start | bytes 552964
  98.5 43.5 %copy-start.49 = (bf16[64,640]{1,0:T(8,128)(2,1)S(1)}, bf16[64,640]{1,0:T(8,128)(2,1)}, u32[]{:S(2)}) copy-start(bf16[64,640]{1,0:T(8,128)(2,1)} %get-tuple-element.69) | copy-start | bytes 245764
  98.5 42.0 %collective-permute-start.19 = (bf16[80,640]{1,0:T(8,128)(2,1)}, bf16[80,640]{1,0:T(8,128)(2,1)S(1)}, u32[]{:S(2)}, u32[]{:S(2)}) collective-permute-start(bf16[80,640]{1,0:T(8,128)(2,1)} %get-tuple-element.68), channel_id=1, source_target_pairs={{0,15},{1,10},{2,9},{3,12},{4,11},{5,14},{6,13},{7,8}} | collective-permute-start | bytes 307208 | tf_op jit(solution)/shard_map/ppermute | solution.py:591
  102.4 50.2 %collective-permute-start.31 = (bf16[80,6144]{1,0:T(8,128)(2,1)}, bf16[80,6144]{1,0:T(8,128)(2,1)S(1)}, u32[]{:S(2)}, u32[]{:S(2)}) collective-permute-start(bf16[80,6144]{1,0:T(8,128)(2,1)} %pack12.1), channel_id=1, source_target_pairs={{8,14},{9,15},{10,12},{11,13},{12,10},{13,11},{14,8},{15,9},{16,22... | collective-permute-start | bytes 2949128 | tf_op jit(solution)/shard_map/ppermute | solution.py:643
  125.8 45.7 %collective-permute-start.30 = (bf16[80,6144]{1,0:T(8,128)(2,1)}, bf16[80,6144]{1,0:T(8,128)(2,1)S(1)}, u32[]{:S(2)}, u32[]{:S(2)}) collective-permute-start(bf16[80,6144]{1,0:T(8,128)(2,1)} %pack12.1), channel_id=1, source_target_pairs={{8,12},{9,13},{10,14},{11,15},{12,8},{13,9},{14,10},{15,11},{16,20... | collective-permute-start | bytes 2949128 | tf_op jit(solution)/shard_map/ppermute | solution.py:643
  132.8 38.7 %collective-permute-start.29 = (bf16[80,6144]{1,0:T(8,128)(2,1)}, bf16[80,6144]{1,0:T(8,128)(2,1)S(1)}, u32[]{:S(2)}, u32[]{:S(2)}) collective-permute-start(bf16[80,6144]{1,0:T(8,128)(2,1)} %pack12.1), channel_id=1, source_target_pairs={{8,10},{9,11},{10,8},{11,9},{12,14},{13,15},{14,12},{15,13},{16,18... | collective-permute-start | bytes 2949128 | tf_op jit(solution)/shard_map/ppermute | solution.py:643
  139.9 2.1 collective-permute-start.22
  140.6 0.7 collective-permute-start.18
  141.3 1.4 collective-permute-start.21
  142.0 1.4 collective-permute-start.20
  142.8 0.7 collective-permute-start.23
  175.2 11.6 %collective-permute-start.32 = (bf16[4,80,6144]{2,1,0:T(8,128)(2,1)S(1)}, bf16[4,80,6144]{2,1,0:T(8,128)(2,1)S(1)}, u32[]{:S(2)}, u32[]{:S(2)}) collective-permute-start(bf16[4,80,6144]{2,1,0:T(8,128)(2,1)S(1)} %pad_maximum_fusion.rest_1_.rest_0_), channel_id=1, source_target_pairs={{8,9},{9,8},{10,11},{11,10},{12,13},{13,12},{14,15},{15,14},{16,17... | collective-permute-start | bytes 11796488 | tf_op jit(solution)/shard_map/ppermute | solution.py:643
  180.4 2.7 collective-permute-start.24
  181.1 2.1 collective-permute-start.27
  181.8 1.4 collective-permute-start.26
  182.4 1.7 collective-permute-start.25
  183.3 0.9 collective-permute-start.28
  196.7 15.4 %collective-permute-start.34 = (bf16[80,640]{1,0:T(8,128)(2,1)}, bf16[80,640]{1,0:T(8,128)(2,1)S(1)}, u32[]{:S(2)}, u32[]{:S(2)}) collective-permute-start(bf16[80,640]{1,0:T(8,128)(2,1)} %get-tuple-element.83), channel_id=1, source_target_pairs={{8,23},{9,18},{10,17},{11,20},{12,19},{13,22},{14,21},{15,16}} | collective-permute-start | bytes 307208 | tf_op jit(solution)/shard_map/ppermute | solution.py:591
  198.0 32.4 %collective-permute-start.37 = (f32[8,640]{1,0:T(8,128)}, f32[8,640]{1,0:T(8,128)S(1)}, u32[]{:S(2)}, u32[]{:S(2)}) collective-permute-start(f32[8,640]{1,0:T(8,128)} %get-tuple-element.85), channel_id=1, source_target_pairs={{8,20},{9,21},{10,22},{11,23},{12,16},{13,17},{14,18},{15,19}} | collective-permute-start | bytes 61448 | tf_op jit(solution)/shard_map/ppermute | solution.py:591
  199.3 31.1 %collective-permute-start.36 = (f32[8,640]{1,0:T(8,128)}, f32[8,640]{1,0:T(8,128)S(1)}, u32[]{:S(2)}, u32[]{:S(2)}) collective-permute-start(f32[8,640]{1,0:T(8,128)} %get-tuple-element.85), channel_id=1, source_target_pairs={{8,18},{9,23},{10,20},{11,17},{12,22},{13,19},{14,16},{15,21}} | collective-permute-start | bytes 61448 | tf_op jit(solution)/shard_map/ppermute | solution.py:591
  200.6 31.9 %collective-permute-start.35 = (bf16[64,640]{1,0:T(8,128)(2,1)}, bf16[64,640]{1,0:T(8,128)(2,1)S(1)}, u32[]{:S(2)}, u32[]{:S(2)}) collective-permute-start(bf16[64,640]{1,0:T(8,128)(2,1)} %get-tuple-element.84), channel_id=1, source_target_pairs={{8,17},{9,16},{10,19},{11,18},{12,21},{13,20},{14,23},{15,22}} | collective-permute-start | bytes 245768 | tf_op jit(solution)/shard_map/ppermute | solution.py:591
  201.9 28.4 %collective-permute-start.33 = (bf16[144,640]{1,0:T(8,128)(2,1)}, bf16[144,640]{1,0:T(8,128)(2,1)S(1)}, u32[]{:S(2)}, u32[]{:S(2)}) collective-permute-start(bf16[144,640]{1,0:T(8,128)(2,1)} %get-tuple-element.82), channel_id=1, source_target_pairs={{8,16},{9,17},{10,18},{11,19},{12,20},{13,21},{14,22},{15,23}} | collective-permute-start | bytes 552968 | tf_op jit(solution)/shard_map/ppermute | solution.py:591
  230.5 3.2 collective-permute-start.38
  242.3 12.6 %collective-permute-start.39 = (bf16[80,640]{1,0:T(8,128)(2,1)}, bf16[80,640]{1,0:T(8,128)(2,1)S(1)}, u32[]{:S(2)}, u32[]{:S(2)}) collective-permute-start(bf16[80,640]{1,0:T(8,128)(2,1)} %get-tuple-element.87), channel_id=1, source_target_pairs={{16,23},{17,18},{18,17},{19,20},{20,19},{21,22},{22,21},{23,16}} | collective-permute-start | bytes 307208 | tf_op jit(solution)/shard_map/ppermute | solution.py:591
  244.5 36.5 %collective-permute-start.47 = (bf16[768,320]{0,1:T(8,128)(2,1)S(1)}, bf16[768,320]{0,1:T(8,128)(2,1)S(1)}, u32[]{:S(2)}, u32[]{:S(2)}) collective-permute-start(bf16[768,320]{0,1:T(8,128)(2,1)S(1)} %copy.13), channel_id=1, source_target_pairs={{0,24},{1,25},{2,26},{3,27},{4,28},{5,29},{6,30},{7,31}} | collective-permute-start | bytes 1474568 | tf_op jit(solution)/shard_map/ppermute | solution.py:591
  245.2 9.8 %collective-permute-start.42 = (f32[8,640]{1,0:T(8,128)}, f32[8,640]{1,0:T(8,128)S(1)}, u32[]{:S(2)}, u32[]{:S(2)}) collective-permute-start(f32[8,640]{1,0:T(8,128)} %get-tuple-element.89), channel_id=1, source_target_pairs={{16,20},{17,21},{18,22},{19,23},{20,16},{21,17},{22,18},{23,19}} | collective-permute-start | bytes 61448 | tf_op jit(solution)/shard_map/ppermute | solution.py:591
  248.9 6.8 %collective-permute-start.41 = (f32[8,640]{1,0:T(8,128)}, f32[8,640]{1,0:T(8,128)S(1)}, u32[]{:S(2)}, u32[]{:S(2)}) collective-permute-start(f32[8,640]{1,0:T(8,128)} %get-tuple-element.89), channel_id=1, source_target_pairs={{16,18},{17,23},{18,20},{19,17},{20,22},{21,19},{22,16},{23,21}} | collective-permute-start | bytes 61448 | tf_op jit(solution)/shard_map/ppermute | solution.py:591
  252.2 6.2 %collective-permute-start.40 = (bf16[64,640]{1,0:T(8,128)(2,1)}, bf16[64,640]{1,0:T(8,128)(2,1)S(1)}, u32[]{:S(2)}, u32[]{:S(2)}) collective-permute-start(bf16[64,640]{1,0:T(8,128)(2,1)} %get-tuple-element.88), channel_id=1, source_target_pairs={{16,17},{17,16},{18,19},{19,18},{20,21},{21,20},{22,23},{23,22}} | collective-permute-start | bytes 245768 | tf_op jit(solution)/shard_map/ppermute | solution.py:591
  256.5 3.1 collective-permute-start.43
  268.1 15.0 %collective-permute-start.44 = (bf16[144,640]{1,0:T(8,128)(2,1)}, bf16[144,640]{1,0:T(8,128)(2,1)S(1)}, u32[]{:S(2)}, u32[]{:S(2)}) collective-permute-start(bf16[144,640]{1,0:T(8,128)(2,1)} %get-tuple-element.90), channel_id=1, source_target_pairs={{16,24},{17,25},{18,26},{19,27},{20,28},{21,29},{22,30},{23,31}} | collective-permute-start | bytes 552968 | tf_op jit(solution)/shard_map/ppermute | solution.py:591
  269.4 13.7 %collective-permute-start.45 = (bf16[80,640]{1,0:T(8,128)(2,1)}, bf16[80,640]{1,0:T(8,128)(2,1)S(1)}, u32[]{:S(2)}, u32[]{:S(2)}) collective-permute-start(bf16[80,640]{1,0:T(8,128)(2,1)} %get-tuple-element.91), channel_id=1, source_target_pairs={{16,31},{17,26},{18,25},{19,28},{20,27},{21,30},{22,29},{23,24}} | collective-permute-start | bytes 307208 | tf_op jit(solution)/shard_map/ppermute | solution.py:591
  274.2 8.9 %collective-permute-start.46 = (bf16[64,640]{1,0:T(8,128)(2,1)}, bf16[64,640]{1,0:T(8,128)(2,1)S(1)}, u32[]{:S(2)}, u32[]{:S(2)}) collective-permute-start(bf16[64,640]{1,0:T(8,128)(2,1)} %get-tuple-element.92), channel_id=1, source_target_pairs={{16,25},{17,24},{18,27},{19,26},{20,29},{21,28},{22,31},{23,30}} | collective-permute-start | bytes 245768 | tf_op jit(solution)/shard_map/ppermute | solution.py:591
  294.5 2.0 collective-permute-start.51
  295.2 1.4 collective-permute-start.52
  295.8 0.7 collective-permute-start.50
  297.3 2.0 collective-permute-start.53
  298.0 2.0 collective-permute-start.49
  298.7 1.4 collective-permute-start.48
  310.8 2.7 collective-permute-start.54
  311.4 2.1 collective-permute-start.57
  312.1 1.4 collective-permute-start.56
  312.8 2.4 collective-permute-start.55
  314.3 0.9 collective-permute-start.58
  324.2 50.7 %collective-permute-start.59 = (bf16[8,16,320]{2,1,0:T(8,128)(2,1)}, bf16[8,16,320]{2,1,0:T(8,128)(2,1)S(1)}, u32[]{:S(2)}, u32[]{:S(2)}) collective-permute-start(bf16[8,16,320]{2,1,0:T(8,128)(2,1)} %get-tuple-element.104), channel_id=1, source_target_pairs={{24,0},{25,1},{26,2},{27,3},{28,4},{29,5},{30,6},{31,7}} | collective-permute-start | bytes 245768 | tf_op jit(solution)/shard_map/ppermute | solution.py:591
  360.9 14.0 %collective-permute-start.60 = (bf16[8,16,320]{2,1,0:T(8,128)(2,1)}, bf16[8,16,320]{2,1,0:T(8,128)(2,1)S(1)}, u32[]{:S(2)}, u32[]{:S(2)}) collective-permute-start(bf16[8,16,320]{2,1,0:T(8,128)(2,1)} %get-tuple-element.105), channel_id=1, source_target_pairs={{24,8},{25,9},{26,10},{27,11},{28,12},{29,13},{30,14},{31,15}} | collective-permute-start | bytes 245768 | tf_op jit(solution)/shard_map/ppermute | solution.py:591
  367.9 12.4 %collective-permute-start.61 = (bf16[8,16,320]{2,1,0:T(8,128)(2,1)}, bf16[8,16,320]{2,1,0:T(8,128)(2,1)S(1)}, u32[]{:S(2)}, u32[]{:S(2)}) collective-permute-start(bf16[8,16,320]{2,1,0:T(8,128)(2,1)} %get-tuple-element.106), channel_id=1, source_target_pairs={{24,16},{25,17},{26,18},{27,19},{28,20},{29,21},{30,22},{31,23}} | collective-permute-start | bytes 245768 | tf_op jit(solution)/shard_map/ppermute | solution.py:591
  (51 other events, 314.5 us)

commit v2 on v1

--- a/solution.py
+++ b/solution.py
@@ -1,4 +1,3 @@
-from functools import partial
 import math
 
 import jax
@@ -7,6 +6,7 @@
 from jax.experimental import pallas as pl
 from jax.experimental.pallas import tpu as pltpu
 from jax.sharding import PartitionSpec as P
+
 
 GROUPS = 32
 EPSILON = 1e-05
@@ -73,8 +73,7 @@
 
 
 class Shape:
-    def __init__(self, features, packs, n):
-        self.n = n
+    def __init__(self, features, n):
         self.rows = features.shape[1]
         self.cols = features.shape[2]
         self.half = self.cols // 2
@@ -197,7 +196,7 @@
             image[:, :, begin:end] = jnp.zeros((image.shape[0], image.shape[1], end - begin), BF16)
 
 
-def fine_columns(store, row, width, even, odd):
+def fine_columns(store, row, even, odd):
     half = even.shape[0]
     store(row, 0, half, 0, shifted(odd, 1))
     store(row, 0, half, 1, even)
@@ -228,7 +227,7 @@
     ] + list(extra)
 
 
-def call(body, name, n_smem, n_vmem, n_any, outs, scratch, flops, limit=60 * 1024 * 1024):
+def call(body, n_smem, n_vmem, n_any, outs, scratch, flops, limit=60 * 1024 * 1024):
     specs = (
         [pl.BlockSpec(memory_space=pltpu.SMEM)] * n_smem
         + [pl.BlockSpec(memory_space=pltpu.VMEM)] * n_vmem
@@ -242,7 +241,6 @@
         scratch_shapes=scratch,
         compiler_params=pltpu.CompilerParams(vmem_limit_bytes=limit),
         cost_estimate=pl.CostEstimate(flops=flops, bytes_accessed=4_000_000, transcendentals=0),
-        name=name,
     )
 
 
@@ -263,10 +261,10 @@
         sums = moments_of(x_ref[...].astype(F32))
         emit(flags, out_ref, outer_ref, inner_ref, stats_ref, keep, rows, width, sums)
 
-    return call(body, "prepare", 1, 1, 0, message_outs(rows, width, c, keep), [], 1000)(flags, x)
-
-
-def fine_conv(shape, flags, weights, pieces, got, halo, out_halo, keep, residual=None, name="fine"):
+    return call(body, 1, 1, 0, message_outs(rows, width, c, keep), [], 1000)(flags, x)
+
+
+def fine_conv(shape, flags, weights, pieces, got, halo, out_halo, keep, residual=None):
     rows, width, half, c = shape.rows, shape.cols, shape.half, shape.narrow
     out_rows = rows + 2 * out_halo
     image_rows = out_rows + 2
@@ -294,7 +292,7 @@
             value, outside = ext_row(row + halo - out_halo - 1, block, outer, inner, flags, rows, halo, width)
             value = masked(silu((value - mean) * inv), outside).astype(BF16)
             value = jnp.dot(value, mix, preferred_element_type=F32)
-            fine_columns(store, row, width, value[:half], value[half:])
+            fine_columns(store, row, value[:half], value[half:])
         run_conv(weights, buffer, image, acc, copies, out_rows, width)
         scale = 1.0 / math.sqrt(9 * c)
         if residual is None:
@@ -312,7 +310,7 @@
     outs = message_outs(rows, width, c, keep) if residual is None else [((out_rows * width, c), BF16)]
     args = (flags,) + tuple(got) + (() if residual is None else tuple(residual)) + tuple(pieces)
     flops = 2 * out_rows * width * 9 * c * c
-    return call(body, name, 1, 5 + extra, n_pieces, outs, scratch_of(weights, image_rows, out_rows, width), flops)(*args)
+    return call(body, 1, 5 + extra, n_pieces, outs, scratch_of(weights, image_rows, out_rows, width), flops)(*args)
 
 
 def down_conv(shape, flags, weights, pieces, skip, keep):
@@ -354,10 +352,10 @@
 
     scratch = scratch_of(weights, 2 * (out_rows + 1), out_rows, half)
     outs = message_outs(out_rows, half, shape.wide, keep)
-    return call(body, "down", 1, 1, len(pieces), outs, scratch, 2 * out_rows * half * 9 * c * shape.wide)(flags, skip, *pieces)
-
-
-def coarse_conv(shape, flags, weights, pieces, got, keep, residual=None, name="coarse"):
+    return call(body, 1, 1, len(pieces), outs, scratch, 2 * out_rows * half * 9 * c * shape.wide)(flags, skip, *pieces)
+
+
+def coarse_conv(shape, flags, weights, pieces, got, keep, residual=None):
     rows, width, c = shape.rows // 2, shape.half, shape.wide
     extra = 0 if residual is None else 1
 
@@ -390,7 +388,7 @@
     args = (flags,) + tuple(got) + (() if residual is None else (residual,)) + tuple(pieces)
     outs = message_outs(rows, width, c, keep)
     flops = 2 * rows * width * 9 * c * c
-    return call(body, name, 1, 5 + extra, len(pieces), outs, scratch_of(weights, rows + 2, rows, width), flops)(*args)
+    return call(body, 1, 5 + extra, len(pieces), outs, scratch_of(weights, rows + 2, rows, width), flops)(*args)
 
 
 def up_conv(shape, flags, weights, pieces, got, skip, keep):
@@ -429,7 +427,7 @@
     outs = message_outs(rows, width, c_out, keep) + [((8, c_out), F32)]
     flops = 2 * rows * width * 9 * c * c_out
     scratch = scratch_of(weights, rows + 2, rows, width)
-    return call(body, "up", 1, 4, len(pieces), outs, scratch, flops)(flags, *got, skip, *pieces)
+    return call(body, 1, 4, len(pieces), outs, scratch, flops)(flags, *got, skip, *pieces)
 
 
 def join_conv(shape, flags, weights, pieces, got, skip, skip_sums, keep):
@@ -460,7 +458,7 @@
                     outside = flags[1] != 0 if row == 0 else flags[2] != 0 if row == rows + 1 else None
                 value = masked(silu((value - mean) * inv), outside).astype(BF16)
                 value = jnp.dot(value, mix, preferred_element_type=F32)
-                fine_columns(store, row, width, value[:half], value[half:])
+                fine_columns(store, row, value[:half], value[half:])
         run_conv(weights, buffer, image, acc, copies, rows, width)
         out_ref, outer_ref, inner_ref, stats_ref = outs
         value = (acc[...] * (1.0 / math.sqrt(18 * c))).astype(BF16)
@@ -470,7 +468,7 @@
     outs = message_outs(rows, width, c, keep)
     flops = 2 * rows * width * 18 * c * c
     scratch = scratch_of(weights, rows + 2, rows, width)
-    return call(body, "join", 1, 7, len(pieces), outs, scratch, flops)(flags, *got, skip, skip_sums, *pieces)
+    return call(body, 1, 7, len(pieces), outs, scratch, flops)(flags, *got, skip, skip_sums, *pieces)
 
 
 def pair_terms(sums, count):
@@ -523,7 +521,7 @@
             value, outside = ext_row(row, block, outer, inner, flags, rows, 1, width)
             value = masked(silu((value - mean) * inv), outside).astype(BF16)
             value = jnp.dot(value, mix, preferred_element_type=F32)
-            fine_columns(store, row, width, value[:half], value[half:])
+            fine_columns(store, row, value[:half], value[half:])
         run_conv(weights, buffer, image, acc, copies, rows, width)
         for copy in jcopies:
             copy.wait()
@@ -549,45 +547,49 @@
     flops = 2 * rows * width * 11 * c * c
     extra = [pltpu.VMEM((shape.m, shape.cols_of, shape.lanes), BF16), pltpu.SemaphoreType.DMA((8,))]
     scratch = scratch_of(weights, rows + 2, rows, width, extra)
-    return call(body, "last", 1, 7, len(pieces), outs, scratch, flops)(flags, *got, u, skip, *pieces)
+    return call(body, 1, 7, len(pieces), outs, scratch, flops)(flags, *got, u, skip, *pieces)
 
 
 def pack_blocks(shape, pack, low, high):
-    count, columns = high - low, pack.shape[1]
+    count, columns = high - low, pack.shape[0]
+    first = low * shape.blk // 128 * 128
+    last = min(-(-high * shape.blk // 128) * 128, pack.shape[1])
 
     def body(pack_ref, out_ref, rows, sem):
-        copy = pltpu.make_async_copy(pack_ref.at[low * shape.blk : high * shape.blk, :], rows, sem)
+        copy = pltpu.make_async_copy(pack_ref.at[:, first:last], rows, sem)
         copy.start()
-        left = lax.broadcasted_iota(jnp.int32, (columns, columns), 0)
-        right = lax.broadcasted_iota(jnp.int32, (columns, columns), 1)
-        same = jnp.where(left == right, 1.0, 0.0).astype(BF16)
         copy.wait()
         for block in range(count):
-            part = rows[block * shape.blk : (block + 1) * shape.blk, :]
-            made = lax.dot_general(same, part, (((1,), (1,)), ((), ())), preferred_element_type=F32)
             begin, end = block * shape.lanes, (block + 1) * shape.lanes
-            out_ref[:, begin : begin + shape.blk] = made.astype(BF16)
+            at = (low + block) * shape.blk - first
+            out_ref[:, begin : begin + shape.blk] = rows[:, at : at + shape.blk]
             out_ref[:, begin + shape.blk : end] = jnp.zeros((columns, shape.lanes - shape.blk), BF16)
 
-    scratch = [pltpu.VMEM((count * shape.blk, columns), BF16), pltpu.SemaphoreType.DMA(())]
+    scratch = [pltpu.VMEM((columns, last - first), BF16), pltpu.SemaphoreType.DMA(())]
     outs = [((columns, count * shape.lanes), BF16)]
-    return call(body, f"pack{low}", 0, 0, 1, outs, scratch, 1000)(pack)[0]
+    return call(body, 0, 0, 1, outs, scratch, 1000)(pack)[0]
 
 
 def shards(n, n_section, features, section_packs):
     section_id = lax.axis_index("section")
     w = lax.axis_index("space")
-    shape = Shape(features, section_packs, n)
+    shape = Shape(features, n)
     q_rows = shape.narrow * shape.narrow // shape.wide
     pack = section_packs[0]
     flags = jnp.stack([w % 2, (w == 0).astype(jnp.int32), (w == n - 1).astype(jnp.int32), section_id, w]).astype(jnp.int32)
 
     total = pack.shape[0] // shape.blk
-    cuts = [0, 9 * q_rows // shape.blk, 36 * q_rows // shape.blk, total]
+    cuts = [0, 9 * q_rows // shape.blk, 18 * q_rows // shape.blk, 36 * q_rows // shape.blk, total]
     bounds = list(zip(cuts[:-1], cuts[1:], strict=True))
 
     def permute(value, source, target, move):
+        if source == target:
+            return within(value, range(n_section), move)
         pairs = [(source * n + i, target * n + move(i)) for i in range(n)]
+        return lax.ppermute(value, ("section", "space"), pairs)
+
+    def within(value, planes, move):
+        pairs = [(s * n + i, s * n + move(i)) for s in planes for i in range(n)]
         return lax.ppermute(value, ("section", "space"), pairs)
 
     def to_outer(i):
@@ -638,10 +640,6 @@
         total = mine[:, size:] + other[:, size:]
         return (block, outer, inner, mine[:, :size], other[:, :size]), total
 
-    def within(value, planes, move):
-        pairs = [(s * n + i, s * n + move(i)) for s in planes for i in range(n)]
-        return lax.ppermute(value, ("section", "space"), pairs)
-
     def owner_near(flags, j):
         return ((flags[4] // 2) ^ j) * 2 + flags[0]
 
@@ -656,9 +654,12 @@
     def send(number, *deps):
         low, high = bounds[number]
         if n == 8:
-            planes = range(n_section) if number < 2 else range(1, n_section)
-            own = after(pack_blocks(shape, pack, low, high), *deps)
-            return [own] + [within(own, planes, lambda i, k=k: i ^ (2 * k)) for k in range(1, 4)]
+            planes = range(n_section)
+            own = after(pack_blocks(shape, pack.T, low, high), *deps)
+            got = [own]
+            for k in range(1, 4):
+                got.append(within(own, planes, lambda i, k=k: i ^ (2 * k)))
+            return got
         got = lax.all_gather(pack[low * shape.blk : high * shape.blk], "space")
         got = got.reshape(shape.m, n // shape.m, high - low, shape.blk, -1).transpose(0, 1, 4, 2, 3)
         got = got.reshape(shape.m, shape.cols_of, high - low, shape.blk)
@@ -667,13 +668,13 @@
 
     def finish(number, got, *deps):
         if n == 8:
-            near = after(jnp.stack(got), *deps)
-            far = within(near, range(n_section) if number < 2 else range(1, n_section), partner)
+            near = jnp.stack(after(got, *deps))
+            far = within(near, range(n_section), partner)
             pieces[number] = ([near, far], [owner_near, owner_far])
         else:
             pieces[number] = (got, [lambda flags, j: j])
 
-    def weights(start, c_in, c_out, parts):
+    def weights(start, c_in, c_out):
         first = start // shape.blk
         end = (start + 9 * c_in * c_out // shape.wide) // shape.blk
         used = [i for i, (a, b) in enumerate(bounds) if a < end and b > first]
@@ -684,36 +685,38 @@
     x = features[0].reshape(shape.rows, shape.half, 2, narrow).transpose(0, 2, 1, 3).reshape(-1, narrow)
     sent = send(0)
     first = exchange(prepare(shape, flags, after(x, sent[0]), 1), 0, 0)
-    finish(0, sent)
+    finish(0, sent, first[3])
     sent = send(1, sent, first)
-    hidden = fine_conv(shape, flags, *weights(0, narrow, narrow, (narrow,)), first, 1, 0, 2, name="c00")
+    first = (after(first[0], sent[0]),) + first[1:]
+    hidden = fine_conv(shape, flags, *weights(0, narrow, narrow), first, 1, 0, 2)
     second = exchange(hidden, 0, 0)
-    finish(1, sent, second)
-    sent = send(2, sent, pieces[1][0])
-    (skip,) = fine_conv(
-        shape, flags, *weights(9 * q_rows, narrow, narrow, (narrow,)), second, 2, 1, 0, residual=first[:3], name="c01"
-    )
-    coarse = down_conv(shape, flags, *weights(18 * q_rows, narrow, wide, (narrow,)), skip, 1)
+    finish(1, sent, second[3])
+    sent = send(2, sent, second)
+    second = (after(second[0], sent[0]),) + second[1:]
+    (skip,) = fine_conv(shape, flags, *weights(9 * q_rows, narrow, narrow), second, 2, 1, 0, residual=first[:3])
+    finish(2, sent, skip)
+    sent = send(3, sent)
+    skip = after(skip, sent[0])
+    coarse = down_conv(shape, flags, *weights(18 * q_rows, narrow, wide), skip, 1)
     for section in (1, 2):
         got = exchange(coarse, section - 1, section)
         if section == 1:
             skip, got = lax.optimization_barrier((skip, got))
-            skip = permute(skip, 0, 3, lambda i: i)
-        hidden = coarse_conv(shape, flags, *weights(0, wide, wide, (wide,)), got, 1, name=f"c{section}0")
+            last = n_section - 1
+            pairs = [(s * n + i, (last - s if s in (0, last) else s) * n + i) for s in range(n_section) for i in range(n)]
+            skip = lax.ppermute(skip, ("section", "space"), pairs)
+        hidden = coarse_conv(shape, flags, *weights(0, wide, wide), got, 1)
         if section == 1:
-            finish(2, sent, hidden[3])
+            finish(3, sent, hidden[3])
+            hidden, skip = lax.optimization_barrier((hidden, skip))
         then = exchange(hidden, section, section)
-        coarse = coarse_conv(
-            shape, flags, *weights(36 * q_rows, wide, wide, (wide,)), then, 1, residual=got[0], name=f"c{section}1"
-        )
+        coarse = coarse_conv(shape, flags, *weights(36 * q_rows, wide, wide), then, 1, residual=got[0])
     got = exchange(coarse, 2, 3, with_stats=False)
-    *up, skip_stats = up_conv(shape, flags, *weights(0, wide, narrow, (wide,)), got, skip, 1)
+    *up, skip_stats = up_conv(shape, flags, *weights(0, wide, narrow), got, skip, 1)
     got, skip_sums = exchange(up, 3, 3, extra_stats=skip_stats)
-    hidden = join_conv(shape, flags, *weights(18 * q_rows, wide, narrow, (narrow, narrow)), got, skip, skip_sums, 1)
+    hidden = join_conv(shape, flags, *weights(18 * q_rows, wide, narrow), got, skip, skip_sums, 1)
     then = exchange(hidden, 3, 3)
-    outs = last_conv(
-        shape, flags, *weights(36 * q_rows, narrow, narrow, (narrow,)), then, got[0], skip, 45 * q_rows, n_section
-    )
+    outs = last_conv(shape, flags, *weights(36 * q_rows, narrow, narrow), then, got[0], skip, 45 * q_rows, n_section)
     result = jnp.where(section_id == 3, outs[3], jnp.zeros_like(outs[3]))
     for target in range(3):
         result = result + permute(outs[target], 3, target, lambda i: i)

time: 388 us -> 293 us (0.76)
  starting transfers between devices: 158 us -> 58.9 us
  waiting for transfers between devices: 104 us -> 112 us
  local copies, waits for them, and re-layouts: 17.6 us -> 12.3 us
    ppermute x50 -> x16, starting transfers between devices: 108 us -> 22.3 us  [permute(): return lax.ppermute(value, ('section', 'space'), pairs)]
    ppermute x12 -> x49, waiting for transfers between devices: 66.9 us -> 90.9 us  [within(): return lax.ppermute(value, ('section', 'space'), pairs)]
    ppermute x50 -> x16, waiting for transfers between devices: 36.7 us -> 21.2 us  [permute(): return lax.ppermute(value, ('section', 'space'), pairs)]
    ppermute x12 -> x49, starting transfers between devices: 49.9 us -> 35.9 us  [within(): return lax.ppermute(value, ('section', 'space'), pairs)]
    unnamed x108 -> x105, local copies, waits for them, and re-layouts: 13.9 us -> 8.64 us
    pallas_call x14 -> x15, Pallas kernels: 90.5 us -> 91.3 us  [the longest x4 31.8 us: coarse_conv(): call(body, 1, 5 + extra, len(pieces), outs, scratch_of(weights, rows + 2,...]
  transfers between devices with their start and end apart: 62 -> 66, of which waited for: 15 -> 33; matrix products, arithmetic and copies ran while one was open for 2% -> 2% of each run, Pallas kernels for 6% -> 8%
where the time goes in v2:
time: 293 us; the launch traced here: 287 us
  waiting for transfers between devices  112 us (38%)
  Pallas kernels  91.3 us (31%)
  starting transfers between devices  58.9 us (20%)
  local copies, waits for them, and re-layouts  12.3 us (4%)
  other arithmetic  11.1 us (4%)
    ppermute x49, waiting for transfers between devices, within(): return lax.ppermute(value, ('section', 'space'), pairs)  90.9 us
    ppermute x49, starting transfers between devices, within(): return lax.ppermute(value, ('section', 'space'), pairs)  35.9 us
    pallas_call x4, Pallas kernels, coarse_conv(): call(body, 1, 5 + extra, len(pieces), outs, scratch_of(weights, rows + 2,...  31.8 us
    ppermute x16, starting transfers between devices, permute(): return lax.ppermute(value, ('section', 'space'), pairs)  22.3 us
    ppermute x16, waiting for transfers between devices, permute(): return lax.ppermute(value, ('section', 'space'), pairs)  21.2 us
    pallas_call x2, Pallas kernels, fine_conv(): call(body, 1, 5 + extra, n_pieces, outs, scratch_of(weights, image_rows,...  15.6 us
    pallas_call x1, Pallas kernels, join_conv(): call(body, 1, 7, len(pieces), outs, scratch, flops)  10.1 us
    pallas_call x1, Pallas kernels, up_conv(): call(body, 1, 4, len(pieces), outs, scratch, flops)  9.21 us
  transfers between devices with their start and end apart: 66, of which 33 were waited for; matrix products, arithmetic and copies ran while one was open for 2% of the time, Pallas kernels for 8%

profile of v2, /device:TPU:16, one launch (start us, length us, event | category | flops | bytes accessed | tf_op | source)
XLA Modules:
  0.0 286.9 jit_solution(18247569720941167910)
XLA Ops:
  0.0 1.8 shard_map.28
  3.6 2.0 shard_map.29
  5.6 1.9 collective-permute-start.3
  8.6 2.3 collective-permute-start
  12.3 10.1 %collective-permute-done.6 = f32[8,320]{1,0:T(8,128)S(1)} collective-permute-done((f32[8,320]{1,0:T(8,128)}, f32[8,320]{1,0:T(8,128)S(1)}, u32[]{:S(2)}, u32[]{:S(2)}) %collective-permute-start.6) | collective-permute-done | bytes 10272 | tf_op jit(solution)/shard_map/ppermute | solution.py:593
  24.6 1.8 shard_map.30
  28.3 7.2 %shard_map.31 = (bf16[528,320]{1,0:T(8,128)(2,1)}, bf16[272,320]{1,0:T(8,128)(2,1)}, bf16[256,320]{1,0:T(8,128)(2,1)}, f32[8,320]{1,0:T(8,128)}) custom-call(s32[5]{0:T(128)} %stack.91.flags, bf16[528,320]{1,0:T(8,128)(2,1)} %get-tuple-element.85.block.rest_0_, bf16[144,320]{1,0:T(8,128)(2,1)} %copy-done.37, bf16[128,320]{1,0:T(8,128)(2,1)} %copy-done.45, ...), custom_call_target="tpu_custom_call" | custom-call | flops 943718400 | bytes 4000000 | tf_op jit(solution)/shard_map/pallas_call | solution.py:313
  35.5 1.4 collective-permute-start.12
  37.4 1.4 collective-permute-start.10
  38.8 1.6 collective-permute-start.9
  40.4 1.1 collective-permute-start.15
  41.4 2.8 collective-permute-done.12.outer
  44.8 8.5 %collective-permute-done.15 = f32[8,320]{1,0:T(8,128)S(1)} collective-permute-done((f32[8,320]{1,0:T(8,128)}, f32[8,320]{1,0:T(8,128)S(1)}, u32[]{:S(2)}, u32[]{:S(2)}) %collective-permute-start.15) | collective-permute-done | bytes 10272 | tf_op jit(solution)/shard_map/ppermute | solution.py:593
  55.6 2.0 shard_map.32
  57.9 1.7 collective-permute-start.20
  62.4 8.4 %shard_map.33.skip_ref = bf16[768,320]{1,0:T(8,128)(2,1)} custom-call(s32[5]{0:T(128)} %stack.91.flags, bf16[528,320]{1,0:T(8,128)(2,1)} %get-tuple-element.95.block, bf16[272,320]{1,0:T(8,128)(2,1)} %copy-done.38, bf16[256,320]{1,0:T(8,128)(2,1)} %copy-done.40, f32[8,320]{1,0:T(8,128)} %copy-done.35, f32[8,320]{1,0:T(8,128)} %copy-done.50, ...), custom_call_target="tpu_custom_call" | custom-call | flops 1415577600 | bytes 4000000 | tf_op jit(solution)/shard_map/pallas_call | solution.py:313
  70.8 2.5 collective-permute-done.20
  73.3 9.8 %collective-permute-done.19 = bf16[80,3072]{1,0:T(8,128)(2,1)} collective-permute-done((bf16[80,3072]{1,0:T(8,128)(2,1)}, bf16[80,3072]{1,0:T(8,128)(2,1)}, u32[]{:S(2)}, u32[]{:S(2)}) %collective-permute-start.19) | collective-permute-done | bytes 491552 | tf_op jit(solution)/shard_map/ppermute | solution.py:593
  84.0 1.6 pad_maximum_fusion.1.rest_0_.rest_4_
  85.7 3.1 %shard_map.34 = bf16[80,6144]{1,0:T(8,128)(2,1)} custom-call(bf16[80,11520]{1,0:T(8,128)(2,1)} %bitcast.34), custom_call_target="tpu_custom_call" | custom-call | flops 1000 | bytes 4000000 | tf_op jit(solution)/shard_map/pallas_call | solution.py:570
  89.7 5.5 %shard_map.35 = (bf16[144,640]{1,0:T(8,128)(2,1)}, bf16[80,640]{1,0:T(8,128)(2,1)}, bf16[64,640]{1,0:T(8,128)(2,1)}, f32[8,640]{1,0:T(8,128)}) custom-call(s32[5]{0:T(128)} %stack.91.flags, bf16[768,320]{1,0:T(8,128)(2,1)} %shard_map.33.skip_ref, bf16[4,80,3072]{2,1,0:T(8,128)(2,1)} %copy-done, bf16[4,80,3072]{2,1,0:T(8,128)(2,1)} %collective-permute-done.21.rest_1_.rest_5_), custom_call_target="tpu_custom_call" | custom-call | flops 471859200 | bytes 4000000 | tf_op jit(solution)/shard_map/pallas_call | solution.py:355
  96.0 1.6 collective-permute-start.36
  98.5 1.0 collective-permute-start.34
  102.5 1.2 collective-permute-done.27.sb
  104.3 8.0 %shard_map.36 = (bf16[144,640]{1,0:T(8,128)(2,1)}, bf16[80,640]{1,0:T(8,128)(2,1)}, bf16[64,640]{1,0:T(8,128)(2,1)}, f32[8,640]{1,0:T(8,128)}) custom-call(s32[5]{0:T(128)} %stack.91.flags, bf16[144,640]{1,0:T(8,128)(2,1)} %copy-done.10, bf16[80,640]{1,0:T(8,128)(2,1)} %copy-done.14, bf16[64,640]{1,0:T(8,128)(2,1)} %copy-done.23, f32[8,640]{1,0:T(8,128)} %copy-done.26, ...), custom_call_target="tpu_custom_call" | custom-call | flops 943718400 | bytes 4000000 | tf_op jit(solution)/shard_map/pallas_call | solution.py:391
  112.2 9.4 %collective-permute-done.36 = bf16[80,6144]{1,0:T(8,128)(2,1)S(1)} collective-permute-done((bf16[80,6144]{1,0:T(8,128)(2,1)S(1)}, bf16[80,6144]{1,0:T(8,128)(2,1)S(1)}, u32[]{:S(2)}, u32[]{:S(2)}) %collective-permute-start.36) | collective-permute-done | bytes 983072 | tf_op jit(solution)/shard_map/ppermute | solution.py:593
  121.6 20.3 %collective-permute-done.35 = bf16[80,6144]{1,0:T(8,128)(2,1)} collective-permute-done((bf16[80,6144]{1,0:T(8,128)(2,1)S(1)}, bf16[80,6144]{1,0:T(8,128)(2,1)}, u32[]{:S(2)}, u32[]{:S(2)}) %collective-permute-start.35) | collective-permute-done | bytes 983072 | tf_op jit(solution)/shard_map/ppermute | solution.py:593
  141.9 3.4 %pad_maximum_fusion.rest_1_.rest_0_ = bf16[4,80,6144]{2,1,0:T(8,128)(2,1)} fusion(bf16[1,80,6144]{2,1,0:T(8,128)(2,1)S(1)} %bitcast.39, bf16[1,80,6144]{2,1,0:T(8,128)(2,1)} %bitcast.25, bf16[1,80,6144]{2,1,0:T(8,128)(2,1)} %bitcast.24, bf16[1,80,6144]{2,1,0:T(8,128)(2,1)S(1)} %bitcast.35), kind=kLoop, calls=%fused_computation | loop fusion | flops 5898240 | bytes 7864320 | tf_op jit(solution)/shard_map/stack | solution.py:671
  146.3 1.7 collective-permute-start.29
  150.3 1.7 collective-permute-done.29.outer
  152.0 1.7 collective-permute-done.31
  153.9 1.2 collective-permute-done.33.sb
  155.7 7.9 %shard_map.37 = (bf16[144,640]{1,0:T(8,128)(2,1)}, bf16[80,640]{1,0:T(8,128)(2,1)}, bf16[64,640]{1,0:T(8,128)(2,1)}, f32[8,640]{1,0:T(8,128)}) custom-call(s32[5]{0:T(128)} %stack.91.flags, bf16[144,640]{1,0:T(8,128)(2,1)} %get-tuple-element.120.block, bf16[80,640]{1,0:T(8,128)(2,1)} %copy-done.16, bf16[64,640]{1,0:T(8,128)(2,1)} %copy-done.21, ...), custom_call_target="tpu_custom_call" | custom-call | flops 943718400 | bytes 4000000 | tf_op jit(solution)/shard_map/pallas_call | solution.py:391
  163.6 1.3 collective-permute-start.39
  164.9 1.3 collective-permute-start.42
  166.2 1.3 collective-permute-start.41
  167.5 1.3 collective-permute-start.40
  168.8 1.3 collective-permute-start.38
  170.1 2.6 collective-permute-done.39.outer
  172.7 6.9 %collective-permute-done.38.block.rest_0_ = bf16[144,640]{1,0:T(8,128)(2,1)S(1)} collective-permute-done((bf16[144,640]{1,0:T(8,128)(2,1)}, bf16[144,640]{1,0:T(8,128)(2,1)S(1)}, u32[]{:S(2)}, u32[]{:S(2)}) %collective-permute-start.38) | collective-permute-done | bytes 184352 | tf_op jit(solution)/shard_map/ppermute | solution.py:589
  179.8 1.2 collective-permute-done.43.sb
  181.5 8.0 %shard_map.38 = (bf16[144,640]{1,0:T(8,128)(2,1)}, bf16[80,640]{1,0:T(8,128)(2,1)}, bf16[64,640]{1,0:T(8,128)(2,1)}, f32[8,640]{1,0:T(8,128)}) custom-call(s32[5]{0:T(128)} %stack.91.flags, bf16[144,640]{1,0:T(8,128)(2,1)} %copy-done.11, bf16[80,640]{1,0:T(8,128)(2,1)} %copy-done.15, bf16[64,640]{1,0:T(8,128)(2,1)} %copy-done.20, f32[8,640]{1,0:T(8,128)} %copy-done.27, ...), custom_call_target="tpu_custom_call" | custom-call | flops 943718400 | bytes 4000000 | tf_op jit(solution)/shard_map/pallas_call | solution.py:391
  190.5 1.1 collective-permute-start.47
  193.0 2.7 collective-permute-done.44.outer
  197.4 1.2 collective-permute-done.48.sb
  199.1 7.9 %shard_map.39 = (bf16[144,640]{1,0:T(8,128)(2,1)}, bf16[80,640]{1,0:T(8,128)(2,1)}, bf16[64,640]{1,0:T(8,128)(2,1)}, f32[8,640]{1,0:T(8,128)}) custom-call(s32[5]{0:T(128)} %stack.91.flags, bf16[144,640]{1,0:T(8,128)(2,1)} %get-tuple-element.132.block, bf16[80,640]{1,0:T(8,128)(2,1)} %copy-done.17, bf16[64,640]{1,0:T(8,128)(2,1)} %copy-done.22, ...), custom_call_target="tpu_custom_call" | custom-call | flops 943718400 | bytes 4000000 | tf_op jit(solution)/shard_map/pallas_call | solution.py:391
  207.0 6.6 %collective-permute-start.49 = (bf16[144,640]{1,0:T(8,128)(2,1)}, bf16[144,640]{1,0:T(8,128)(2,1)S(1)}, u32[]{:S(2)}, u32[]{:S(2)}) collective-permute-start(bf16[144,640]{1,0:T(8,128)(2,1)} %get-tuple-element.136), channel_id=1, source_target_pairs={{16,24},{17,25},{18,26},{19,27},{20,28},{21,29},{22,30},{23,31}} | collective-permute-start | bytes 552968 | tf_op jit(solution)/shard_map/ppermute | solution.py:589
  213.6 1.8 collective-permute-start.50
  215.4 1.5 collective-permute-start.51
  216.9 1.1 copy.11.skip_ref
  218.0 4.0 %collective-permute-done.51.inner = bf16[64,640]{1,0:T(8,128)(2,1)S(1)} collective-permute-done((bf16[64,640]{1,0:T(8,128)(2,1)}, bf16[64,640]{1,0:T(8,128)(2,1)S(1)}, u32[]{:S(2)}, u32[]{:S(2)}) %collective-permute-start.51) | collective-permute-done | bytes 81952 | tf_op jit(solution)/shard_map/ppermute | solution.py:589
  223.4 9.2 %shard_map.40 = (bf16[528,320]{1,0:T(8,128)(2,1)}, bf16[144,320]{1,0:T(8,128)(2,1)}, bf16[128,320]{1,0:T(8,128)(2,1)}, f32[8,320]{1,0:T(8,128)}, f32[8,320]{1,0:T(8,128)}) custom-call(s32[5]{0:T(128)} %stack.91.flags, bf16[144,640]{1,0:T(8,128)(2,1)} %copy-done.41, bf16[80,640]{1,0:T(8,128)(2,1)} %copy-done.44, bf16[64,640]{1,0:T(8,128)(2,1)} %copy-done.49, ...), custom_call_target="tpu_custom_call" | custom-call | flops 1887436800 | bytes 4000000 | tf_op jit(solution)/shard_map/pallas_call | solution.py:430
  233.4 1.0 collective-permute-start.55
  235.3 2.8 collective-permute-done.55
  238.3 1.3 collective-permute-done.54
  242.5 4.6 %collective-permute-done.52.outer = bf16[144,320]{1,0:T(8,128)(2,1)S(1)} collective-permute-done((bf16[144,320]{1,0:T(8,128)(2,1)}, bf16[144,320]{1,0:T(8,128)(2,1)S(1)}, u32[]{:S(2)}, u32[]{:S(2)}) %collective-permute-start.52) | collective-permute-done | bytes 92192 | tf_op jit(solution)/shard_map/ppermute | solution.py:593
  247.8 10.1 %shard_map.41 = (bf16[528,320]{1,0:T(8,128)(2,1)}, bf16[144,320]{1,0:T(8,128)(2,1)}, bf16[128,320]{1,0:T(8,128)(2,1)}, f32[8,320]{1,0:T(8,128)}) custom-call(s32[5]{0:T(128)} %stack.91.flags, bf16[528,320]{1,0:T(8,128)(2,1)} %get-tuple-element.140.block.u_ref, bf16[144,320]{1,0:T(8,128)(2,1)} %copy-done.42, bf16[128,320]{1,0:T(8,128)(2,1)} %copy-done.47, ...), custom_call_target="tpu_custom_call" | custom-call | flops 1887436800 | bytes 4000000 | tf_op jit(solution)/shard_map/pallas_call | solution.py:471
  258.1 1.3 collective-permute-start.61
  260.2 1.5 collective-permute-start.59
  261.7 1.8 collective-permute-done.58.outer
  265.3 1.1 collective-permute-done.62.sb
  267.0 8.4 %shard_map.42 = (bf16[8,16,320]{2,1,0:T(8,128)(2,1)}, bf16[8,16,320]{2,1,0:T(8,128)(2,1)}, bf16[8,16,320]{2,1,0:T(8,128)(2,1)}, bf16[8,16,320]{2,1,0:T(8,128)(2,1)}) custom-call(s32[5]{0:T(128)} %stack.91.flags, bf16[528,320]{1,0:T(8,128)(2,1)} %get-tuple-element.145.block, bf16[144,320]{1,0:T(8,128)(2,1)} %copy-done.18, bf16[128,320]{1,0:T(8,128)(2,1)} %copy-done.19, ...), custom_call_target="tpu_custom_call" | custom-call | flops 1153433600 | bytes 4000000 | tf_op jit(solution)/shard_map/pallas_call | solution.py:550
  276.8 1.3 collective-permute-start.65
  278.1 7.7 %collective-permute-done.65 = bf16[8,16,320]{2,1,0:T(8,128)(2,1)S(1)} collective-permute-done((bf16[8,16,320]{2,1,0:T(8,128)(2,1)}, bf16[8,16,320]{2,1,0:T(8,128)(2,1)S(1)}, u32[]{:S(2)}, u32[]{:S(2)}) %collective-permute-start.65) | collective-permute-done | bytes 81952 | tf_op jit(solution)/shard_map/ppermute | solution.py:589
  (229 shorter events, 43.1 us)
Async XLA Ops:
  5.6 6.4 %collective-permute-start.3 = (bf16[144,320]{1,0:T(8,128)(2,1)}, bf16[144,320]{1,0:T(8,128)(2,1)S(1)}, u32[]{:S(2)}, u32[]{:S(2)}) collective-permute-start(bf16[144,320]{1,0:T(8,128)(2,1)} %get-tuple-element.81), channel_id=1, source_target_pairs={{0,7},{1,2},{2,1},{3,4},{4,3},{5,6},{6,5},{7,0},{8,15},{9,10},{10,... | collective-permute-start | bytes 276488 | tf_op jit(solution)/shard_map/ppermute | solution.py:593
  7.5 16.2 %collective-permute-start.2 = (bf16[80,1536]{1,0:T(8,128)(2,1)}, bf16[80,1536]{1,0:T(8,128)(2,1)S(1)}, u32[]{:S(2)}, u32[]{:S(2)}) collective-permute-start(bf16[80,1536]{1,0:T(8,128)(2,1)} %shard_map.28), channel_id=1, source_target_pairs={{0,6},{1,7},{2,4},{3,5},{4,2},{5,3},{6,0},{7,1},{8,14},{9,15},{10,... | collective-permute-start | bytes 737288 | tf_op jit(solution)/shard_map/ppermute | solution.py:593
  8.1 15.6 %collective-permute-start.1 = (bf16[80,1536]{1,0:T(8,128)(2,1)}, bf16[80,1536]{1,0:T(8,128)(2,1)S(1)}, u32[]{:S(2)}, u32[]{:S(2)}) collective-permute-start(bf16[80,1536]{1,0:T(8,128)(2,1)} %shard_map.28), channel_id=1, source_target_pairs={{0,4},{1,5},{2,6},{3,7},{4,0},{5,1},{6,2},{7,3},{8,12},{9,13},{10,... | collective-permute-start | bytes 737288 | tf_op jit(solution)/shard_map/ppermute | solution.py:593
  8.6 15.1 %collective-permute-start = (bf16[80,1536]{1,0:T(8,128)(2,1)}, bf16[80,1536]{1,0:T(8,128)(2,1)S(1)}, u32[]{:S(2)}, u32[]{:S(2)}) collective-permute-start(bf16[80,1536]{1,0:T(8,128)(2,1)} %shard_map.28), channel_id=1, source_target_pairs={{0,2},{1,3},{2,0},{3,1},{4,6},{5,7},{6,4},{7,5},{8,10},{9,11},{10,... | collective-permute-start | bytes 737288 | tf_op jit(solution)/shard_map/ppermute | solution.py:593
  11.0 11.4 %collective-permute-start.6 = (f32[8,320]{1,0:T(8,128)}, f32[8,320]{1,0:T(8,128)S(1)}, u32[]{:S(2)}, u32[]{:S(2)}) collective-permute-start(f32[8,320]{1,0:T(8,128)} %get-tuple-element.83), channel_id=1, source_target_pairs={{0,4},{1,5},{2,6},{3,7},{4,0},{5,1},{6,2},{7,3},{8,12},{9,13},{10,... | collective-permute-start | bytes 30728 | tf_op jit(solution)/shard_map/ppermute | solution.py:593
  12.0 10.9 %collective-permute-start.5 = (f32[8,320]{1,0:T(8,128)}, f32[8,320]{1,0:T(8,128)S(1)}, u32[]{:S(2)}, u32[]{:S(2)}) collective-permute-start(f32[8,320]{1,0:T(8,128)} %get-tuple-element.83), channel_id=1, source_target_pairs={{0,2},{1,7},{2,4},{3,1},{4,6},{5,3},{6,0},{7,5},{8,10},{9,15},{10,... | collective-permute-start | bytes 30728 | tf_op jit(solution)/shard_map/ppermute | solution.py:593
  23.9 2.8 collective-permute-start.8
  24.0 2.7 collective-permute-start.4
  24.5 2.2 collective-permute-start.7
  35.5 8.7 %collective-permute-start.12 = (bf16[272,320]{1,0:T(8,128)(2,1)}, bf16[272,320]{1,0:T(8,128)(2,1)S(1)}, u32[]{:S(2)}, u32[]{:S(2)}) collective-permute-start(bf16[272,320]{1,0:T(8,128)(2,1)} %get-tuple-element.91), channel_id=1, source_target_pairs={{0,7},{1,2},{2,1},{3,4},{4,3},{5,6},{6,5},{7,0},{8,15},{9,10},{10,... | collective-permute-start | bytes 522248 | tf_op jit(solution)/shard_map/ppermute | solution.py:593
  36.9 17.9 %collective-permute-start.11 = (bf16[80,1536]{1,0:T(8,128)(2,1)S(1)}, bf16[80,1536]{1,0:T(8,128)(2,1)S(1)}, u32[]{:S(2)}, u32[]{:S(2)}) collective-permute-start(bf16[80,1536]{1,0:T(8,128)(2,1)S(1)} %copy-done.9), channel_id=1, source_target_pairs={{0,6},{1,7},{2,4},{3,5},{4,2},{5,3},{6,0},{7,1},{8,14},{9,15},{10,... | collective-permute-start | bytes 737288 | tf_op jit(solution)/shard_map/ppermute | solution.py:593
  37.4 17.4 %collective-permute-start.10 = (bf16[80,1536]{1,0:T(8,128)(2,1)S(1)}, bf16[80,1536]{1,0:T(8,128)(2,1)S(1)}, u32[]{:S(2)}, u32[]{:S(2)}) collective-permute-start(bf16[80,1536]{1,0:T(8,128)(2,1)S(1)} %copy-done.9), channel_id=1, source_target_pairs={{0,4},{1,5},{2,6},{3,7},{4,0},{5,1},{6,2},{7,3},{8,12},{9,13},{10,... | collective-permute-start | bytes 737288 | tf_op jit(solution)/shard_map/ppermute | solution.py:593
  38.8 16.0 %collective-permute-start.9 = (bf16[80,1536]{1,0:T(8,128)(2,1)S(1)}, bf16[80,1536]{1,0:T(8,128)(2,1)S(1)}, u32[]{:S(2)}, u32[]{:S(2)}) collective-permute-start(bf16[80,1536]{1,0:T(8,128)(2,1)S(1)} %copy-done.9), channel_id=1, source_target_pairs={{0,2},{1,3},{2,0},{3,1},{4,6},{5,7},{6,4},{7,5},{8,10},{9,11},{10,... | collective-permute-start | bytes 737288 | tf_op jit(solution)/shard_map/ppermute | solution.py:593
  40.4 12.9 %collective-permute-start.15 = (f32[8,320]{1,0:T(8,128)}, f32[8,320]{1,0:T(8,128)S(1)}, u32[]{:S(2)}, u32[]{:S(2)}) collective-permute-start(f32[8,320]{1,0:T(8,128)} %get-tuple-element.93), channel_id=1, source_target_pairs={{0,4},{1,5},{2,6},{3,7},{4,0},{5,1},{6,2},{7,3},{8,12},{9,13},{10,... | collective-permute-start | bytes 30728 | tf_op jit(solution)/shard_map/ppermute | solution.py:593
  44.2 9.8 %collective-permute-start.14 = (f32[8,320]{1,0:T(8,128)}, f32[8,320]{1,0:T(8,128)S(1)}, u32[]{:S(2)}, u32[]{:S(2)}) collective-permute-start(f32[8,320]{1,0:T(8,128)} %get-tuple-element.93), channel_id=1, source_target_pairs={{0,2},{1,7},{2,4},{3,1},{4,6},{5,3},{6,0},{7,5},{8,10},{9,15},{10,... | collective-permute-start | bytes 30728 | tf_op jit(solution)/shard_map/ppermute | solution.py:593
  55.0 6.5 %collective-permute-start.17 = (bf16[4,80,1536]{2,1,0:T(8,128)(2,1)S(1)}, bf16[4,80,1536]{2,1,0:T(8,128)(2,1)S(1)}, u32[]{:S(2)}, u32[]{:S(2)}) collective-permute-start(bf16[4,80,1536]{2,1,0:T(8,128)(2,1)S(1)} %pad_maximum_fusion.3.rest_3_.rest_2_), channel_id=1, source_target_pairs={{0,1},{1,0},{2,3},{3,2},{4,5},{5,4},{6,7},{7,6},{8,9},{9,8},{10,11... | collective-permute-start | bytes 2949128 | tf_op jit(solution)/shard_map/ppermute | solution.py:593
  55.1 2.8 collective-permute-start.13
  55.5 2.4 collective-permute-start.16
  57.9 15.4 %collective-permute-start.20 = (bf16[80,3072]{1,0:T(8,128)(2,1)}, bf16[80,3072]{1,0:T(8,128)(2,1)}, u32[]{:S(2)}, u32[]{:S(2)}) collective-permute-start(bf16[80,3072]{1,0:T(8,128)(2,1)} %shard_map.32), channel_id=1, source_target_pairs={{0,6},{1,7},{2,4},{3,5},{4,2},{5,3},{6,0},{7,1},{8,14},{9,15},{10,... | collective-permute-start | bytes 1474568 | tf_op jit(solution)/shard_map/ppermute | solution.py:593
  59.6 23.5 %collective-permute-start.19 = (bf16[80,3072]{1,0:T(8,128)(2,1)}, bf16[80,3072]{1,0:T(8,128)(2,1)}, u32[]{:S(2)}, u32[]{:S(2)}) collective-permute-start(bf16[80,3072]{1,0:T(8,128)(2,1)} %shard_map.32), channel_id=1, source_target_pairs={{0,4},{1,5},{2,6},{3,7},{4,0},{5,1},{6,2},{7,3},{8,12},{9,13},{10,... | collective-permute-start | bytes 1474568 | tf_op jit(solution)/shard_map/ppermute | solution.py:593
  60.5 22.7 %collective-permute-start.18 = (bf16[80,3072]{1,0:T(8,128)(2,1)}, bf16[80,3072]{1,0:T(8,128)(2,1)S(1)}, u32[]{:S(2)}, u32[]{:S(2)}) collective-permute-start(bf16[80,3072]{1,0:T(8,128)(2,1)} %shard_map.32), channel_id=1, source_target_pairs={{0,2},{1,3},{2,0},{3,1},{4,6},{5,7},{6,4},{7,5},{8,10},{9,11},{10,... | collective-permute-start | bytes 1474568 | tf_op jit(solution)/shard_map/ppermute | solution.py:593
  85.6 4.2 %collective-permute-start.21 = (bf16[4,80,3072]{2,1,0:T(8,128)(2,1)S(1)}, bf16[4,80,3072]{2,1,0:T(8,128)(2,1)}, u32[]{:S(2)}, u32[]{:S(2)}) collective-permute-start(bf16[4,80,3072]{2,1,0:T(8,128)(2,1)S(1)} %pad_maximum_fusion.1.rest_0_.rest_4_), channel_id=1, source_target_pairs={{0,1},{1,0},{2,3},{3,2},{4,5},{5,4},{6,7},{7,6},{8,9},{9,8},{10,11... | collective-permute-start | bytes 5898248 | tf_op jit(solution)/shard_map/ppermute | solution.py:593
  95.3 4.9 %collective-permute-start.23 = (bf16[80,640]{1,0:T(8,128)(2,1)}, bf16[80,640]{1,0:T(8,128)(2,1)S(1)}, u32[]{:S(2)}, u32[]{:S(2)}) collective-permute-start(bf16[80,640]{1,0:T(8,128)(2,1)} %get-tuple-element.107), channel_id=1, source_target_pairs={{0,15},{1,10},{2,9},{3,12},{4,11},{5,14},{6,13},{7,8}} | collective-permute-start | bytes 307208 | tf_op jit(solution)/shard_map/ppermute | solution.py:589
  96.0 25.6 %collective-permute-start.36 = (bf16[80,6144]{1,0:T(8,128)(2,1)S(1)}, bf16[80,6144]{1,0:T(8,128)(2,1)S(1)}, u32[]{:S(2)}, u32[]{:S(2)}) collective-permute-start(bf16[80,6144]{1,0:T(8,128)(2,1)S(1)} %copy-done.5), channel_id=1, source_target_pairs={{0,6},{1,7},{2,4},{3,5},{4,2},{5,3},{6,0},{7,1},{8,14},{9,15},{10,... | collective-permute-start | bytes 2949128 | tf_op jit(solution)/shard_map/ppermute | solution.py:593
  97.6 44.3 %collective-permute-start.35 = (bf16[80,6144]{1,0:T(8,128)(2,1)S(1)}, bf16[80,6144]{1,0:T(8,128)(2,1)}, u32[]{:S(2)}, u32[]{:S(2)}) collective-permute-start(bf16[80,6144]{1,0:T(8,128)(2,1)S(1)} %copy-done.5), channel_id=1, source_target_pairs={{0,4},{1,5},{2,6},{3,7},{4,0},{5,1},{6,2},{7,3},{8,12},{9,13},{10,... | collective-permute-start | bytes 2949128 | tf_op jit(solution)/shard_map/ppermute | solution.py:593
  98.5 43.4 %collective-permute-start.34 = (bf16[80,6144]{1,0:T(8,128)(2,1)S(1)}, bf16[80,6144]{1,0:T(8,128)(2,1)}, u32[]{:S(2)}, u32[]{:S(2)}) collective-permute-start(bf16[80,6144]{1,0:T(8,128)(2,1)S(1)} %copy-done.5), channel_id=1, source_target_pairs={{0,2},{1,3},{2,0},{3,1},{4,6},{5,7},{6,4},{7,5},{8,10},{9,11},{10,... | collective-permute-start | bytes 2949128 | tf_op jit(solution)/shard_map/ppermute | solution.py:593
  99.5 2.1 collective-permute-start.26
  100.9 1.4 collective-permute-start.25
  101.7 0.8 collective-permute-start.24
  102.4 1.2 collective-permute-start.27
  145.3 9.7 %collective-permute-start.37 = (bf16[4,80,6144]{2,1,0:T(8,128)(2,1)}, bf16[4,80,6144]{2,1,0:T(8,128)(2,1)}, u32[]{:S(2)}, u32[]{:S(2)}) collective-permute-start(bf16[4,80,6144]{2,1,0:T(8,128)(2,1)} %pad_maximum_fusion.rest_1_.rest_0_), channel_id=1, source_target_pairs={{0,1},{1,0},{2,3},{3,2},{4,5},{5,4},{6,7},{7,6},{8,9},{9,8},{10,11... | collective-permute-start | bytes 11796488 | tf_op jit(solution)/shard_map/ppermute | solution.py:593
  146.3 5.7 %collective-permute-start.29 = (bf16[80,640]{1,0:T(8,128)(2,1)S(1)}, bf16[80,640]{1,0:T(8,128)(2,1)S(1)}, u32[]{:S(2)}, u32[]{:S(2)}) collective-permute-start(bf16[80,640]{1,0:T(8,128)(2,1)S(1)} %copy-done.43), channel_id=1, source_target_pairs={{0,7},{1,2},{2,1},{3,4},{4,3},{5,6},{6,5},{7,0},{8,15},{9,10},{10,... | collective-permute-start | bytes 307208 | tf_op jit(solution)/shard_map/ppermute | solution.py:593
  148.0 4.0 %collective-permute-start.32 = (f32[8,640]{1,0:T(8,128)S(1)}, f32[8,640]{1,0:T(8,128)S(1)}, u32[]{:S(2)}, u32[]{:S(2)}) collective-permute-start(f32[8,640]{1,0:T(8,128)S(1)} %copy-done.33), channel_id=1, source_target_pairs={{0,4},{1,5},{2,6},{3,7},{4,0},{5,1},{6,2},{7,3},{8,12},{9,13},{10,... | collective-permute-start | bytes 61448 | tf_op jit(solution)/shard_map/ppermute | solution.py:593
  148.9 4.8 %collective-permute-start.31 = (f32[8,640]{1,0:T(8,128)S(1)}, f32[8,640]{1,0:T(8,128)S(1)}, u32[]{:S(2)}, u32[]{:S(2)}) collective-permute-start(f32[8,640]{1,0:T(8,128)S(1)} %copy-done.33), channel_id=1, source_target_pairs={{0,2},{1,7},{2,4},{3,1},{4,6},{5,3},{6,0},{7,5},{8,10},{9,15},{10,... | collective-permute-start | bytes 61448 | tf_op jit(solution)/shard_map/ppermute | solution.py:593
  149.9 4.0 %collective-permute-start.30 = (bf16[64,640]{1,0:T(8,128)(2,1)S(1)}, bf16[64,640]{1,0:T(8,128)(2,1)S(1)}, u32[]{:S(2)}, u32[]{:S(2)}) collective-permute-start(bf16[64,640]{1,0:T(8,128)(2,1)S(1)} %copy-done.48), channel_id=1, source_target_pairs={{0,1},{1,0},{2,3},{3,2},{4,5},{5,4},{6,7},{7,6},{8,9},{9,8},{10,11... | collective-permute-start | bytes 245768 | tf_op jit(solution)/shard_map/ppermute | solution.py:593
  153.8 1.2 collective-permute-start.33
  163.6 9.1 %collective-permute-start.39 = (bf16[80,640]{1,0:T(8,128)(2,1)}, bf16[80,640]{1,0:T(8,128)(2,1)S(1)}, u32[]{:S(2)}, u32[]{:S(2)}) collective-permute-start(bf16[80,640]{1,0:T(8,128)(2,1)} %get-tuple-element.129), channel_id=1, source_target_pairs={{8,23},{9,18},{10,17},{11,20},{12,19},{13,22},{14,21},{15,16}} | collective-permute-start | bytes 307208 | tf_op jit(solution)/shard_map/ppermute | solution.py:589
  164.9 14.7 %collective-permute-start.42 = (f32[8,640]{1,0:T(8,128)}, f32[8,640]{1,0:T(8,128)S(1)}, u32[]{:S(2)}, u32[]{:S(2)}) collective-permute-start(f32[8,640]{1,0:T(8,128)} %get-tuple-element.131), channel_id=1, source_target_pairs={{8,20},{9,21},{10,22},{11,23},{12,16},{13,17},{14,18},{15,19}} | collective-permute-start | bytes 61448 | tf_op jit(solution)/shard_map/ppermute | solution.py:589
  166.2 13.4 %collective-permute-start.41 = (f32[8,640]{1,0:T(8,128)}, f32[8,640]{1,0:T(8,128)S(1)}, u32[]{:S(2)}, u32[]{:S(2)}) collective-permute-start(f32[8,640]{1,0:T(8,128)} %get-tuple-element.131), channel_id=1, source_target_pairs={{8,18},{9,23},{10,20},{11,17},{12,22},{13,19},{14,16},{15,21}} | collective-permute-start | bytes 61448 | tf_op jit(solution)/shard_map/ppermute | solution.py:589
  167.5 12.2 %collective-permute-start.40 = (bf16[64,640]{1,0:T(8,128)(2,1)}, bf16[64,640]{1,0:T(8,128)(2,1)S(1)}, u32[]{:S(2)}, u32[]{:S(2)}) collective-permute-start(bf16[64,640]{1,0:T(8,128)(2,1)} %get-tuple-element.130), channel_id=1, source_target_pairs={{8,17},{9,16},{10,19},{11,18},{12,21},{13,20},{14,23},{15,22}} | collective-permute-start | bytes 245768 | tf_op jit(solution)/shard_map/ppermute | solution.py:589
  168.8 10.8 %collective-permute-start.38 = (bf16[144,640]{1,0:T(8,128)(2,1)}, bf16[144,640]{1,0:T(8,128)(2,1)S(1)}, u32[]{:S(2)}, u32[]{:S(2)}) collective-permute-start(bf16[144,640]{1,0:T(8,128)(2,1)} %get-tuple-element.128), channel_id=1, source_target_pairs={{8,16},{9,17},{10,18},{11,19},{12,20},{13,21},{14,22},{15,23}} | collective-permute-start | bytes 552968 | tf_op jit(solution)/shard_map/ppermute | solution.py:589
  179.7 1.2 collective-permute-start.43
  189.5 6.1 %collective-permute-start.44 = (bf16[80,640]{1,0:T(8,128)(2,1)}, bf16[80,640]{1,0:T(8,128)(2,1)S(1)}, u32[]{:S(2)}, u32[]{:S(2)}) collective-permute-start(bf16[80,640]{1,0:T(8,128)(2,1)} %get-tuple-element.133), channel_id=1, source_target_pairs={{0,7},{1,2},{2,1},{3,4},{4,3},{5,6},{6,5},{7,0},{8,15},{9,10},{10,... | collective-permute-start | bytes 307208 | tf_op jit(solution)/shard_map/ppermute | solution.py:593
  190.5 5.2 %collective-permute-start.47 = (f32[8,640]{1,0:T(8,128)}, f32[8,640]{1,0:T(8,128)S(1)}, u32[]{:S(2)}, u32[]{:S(2)}) collective-permute-start(f32[8,640]{1,0:T(8,128)} %get-tuple-element.135), channel_id=1, source_target_pairs={{0,4},{1,5},{2,6},{3,7},{4,0},{5,1},{6,2},{7,3},{8,12},{9,13},{10,... | collective-permute-start | bytes 61448 | tf_op jit(solution)/shard_map/ppermute | solution.py:593
  191.6 4.9 %collective-permute-start.46 = (f32[8,640]{1,0:T(8,128)}, f32[8,640]{1,0:T(8,128)S(1)}, u32[]{:S(2)}, u32[]{:S(2)}) collective-permute-start(f32[8,640]{1,0:T(8,128)} %get-tuple-element.135), channel_id=1, source_target_pairs={{0,2},{1,7},{2,4},{3,1},{4,6},{5,3},{6,0},{7,5},{8,10},{9,15},{10,... | collective-permute-start | bytes 61448 | tf_op jit(solution)/shard_map/ppermute | solution.py:593
  192.3 5.1 %collective-permute-start.45 = (bf16[64,640]{1,0:T(8,128)(2,1)}, bf16[64,640]{1,0:T(8,128)(2,1)S(1)}, u32[]{:S(2)}, u32[]{:S(2)}) collective-permute-start(bf16[64,640]{1,0:T(8,128)(2,1)} %get-tuple-element.134), channel_id=1, source_target_pairs={{0,1},{1,0},{2,3},{3,2},{4,5},{5,4},{6,7},{7,6},{8,9},{9,8},{10,11... | collective-permute-start | bytes 245768 | tf_op jit(solution)/shard_map/ppermute | solution.py:593
  197.3 1.2 collective-permute-start.48
  207.0 15.0 %collective-permute-start.49 = (bf16[144,640]{1,0:T(8,128)(2,1)}, bf16[144,640]{1,0:T(8,128)(2,1)S(1)}, u32[]{:S(2)}, u32[]{:S(2)}) collective-permute-start(bf16[144,640]{1,0:T(8,128)(2,1)} %get-tuple-element.136), channel_id=1, source_target_pairs={{16,24},{17,25},{18,26},{19,27},{20,28},{21,29},{22,30},{23,31}} | collective-permute-start | bytes 552968 | tf_op jit(solution)/shard_map/ppermute | solution.py:589
  213.6 8.5 %collective-permute-start.50 = (bf16[80,640]{1,0:T(8,128)(2,1)}, bf16[80,640]{1,0:T(8,128)(2,1)S(1)}, u32[]{:S(2)}, u32[]{:S(2)}) collective-permute-start(bf16[80,640]{1,0:T(8,128)(2,1)} %get-tuple-element.137), channel_id=1, source_target_pairs={{16,31},{17,26},{18,25},{19,28},{20,27},{21,30},{22,29},{23,24}} | collective-permute-start | bytes 307208 | tf_op jit(solution)/shard_map/ppermute | solution.py:589
  215.4 6.6 %collective-permute-start.51 = (bf16[64,640]{1,0:T(8,128)(2,1)}, bf16[64,640]{1,0:T(8,128)(2,1)S(1)}, u32[]{:S(2)}, u32[]{:S(2)}) collective-permute-start(bf16[64,640]{1,0:T(8,128)(2,1)} %get-tuple-element.138), channel_id=1, source_target_pairs={{16,25},{17,24},{18,27},{19,26},{20,29},{21,28},{22,31},{23,30}} | collective-permute-start | bytes 245768 | tf_op jit(solution)/shard_map/ppermute | solution.py:589
  233.4 4.7 %collective-permute-start.55 = (f32[8,640]{1,0:T(8,128)S(1)}, f32[8,640]{1,0:T(8,128)S(1)}, u32[]{:S(2)}, u32[]{:S(2)}) collective-permute-start(f32[8,640]{1,0:T(8,128)S(1)} %pad_maximum_fusion.4), channel_id=1, source_target_pairs={{0,2},{1,7},{2,4},{3,1},{4,6},{5,3},{6,0},{7,5},{8,10},{9,15},{10,... | collective-permute-start | bytes 61448 | tf_op jit(solution)/shard_map/ppermute | solution.py:593
  234.4 3.9 %collective-permute-start.56 = (f32[8,640]{1,0:T(8,128)S(1)}, f32[8,640]{1,0:T(8,128)S(1)}, u32[]{:S(2)}, u32[]{:S(2)}) collective-permute-start(f32[8,640]{1,0:T(8,128)S(1)} %pad_maximum_fusion.4), channel_id=1, source_target_pairs={{0,4},{1,5},{2,6},{3,7},{4,0},{5,1},{6,2},{7,3},{8,12},{9,13},{10,... | collective-permute-start | bytes 61448 | tf_op jit(solution)/shard_map/ppermute | solution.py:593
  235.3 4.3 %collective-permute-start.54 = (f32[8,640]{1,0:T(8,128)S(1)}, f32[8,640]{1,0:T(8,128)S(1)}, u32[]{:S(2)}, u32[]{:S(2)}) collective-permute-start(f32[8,640]{1,0:T(8,128)S(1)} %pad_maximum_fusion.4), channel_id=1, source_target_pairs={{0,7},{1,2},{2,1},{3,4},{4,3},{5,6},{6,5},{7,0},{8,15},{9,10},{10,... | collective-permute-start | bytes 61448 | tf_op jit(solution)/shard_map/ppermute | solution.py:593
  240.4 1.4 collective-permute-start.57
  240.5 2.1 collective-permute-start.53
  240.9 6.2 %collective-permute-start.52 = (bf16[144,320]{1,0:T(8,128)(2,1)}, bf16[144,320]{1,0:T(8,128)(2,1)S(1)}, u32[]{:S(2)}, u32[]{:S(2)}) collective-permute-start(bf16[144,320]{1,0:T(8,128)(2,1)} %get-tuple-element.141), channel_id=1, source_target_pairs={{0,7},{1,2},{2,1},{3,4},{4,3},{5,6},{6,5},{7,0},{8,15},{9,10},{10,... | collective-permute-start | bytes 276488 | tf_op jit(solution)/shard_map/ppermute | solution.py:593
  257.9 5.7 %collective-permute-start.58 = (bf16[144,320]{1,0:T(8,128)(2,1)}, bf16[144,320]{1,0:T(8,128)(2,1)S(1)}, u32[]{:S(2)}, u32[]{:S(2)}) collective-permute-start(bf16[144,320]{1,0:T(8,128)(2,1)} %get-tuple-element.146), channel_id=1, source_target_pairs={{0,7},{1,2},{2,1},{3,4},{4,3},{5,6},{6,5},{7,0},{8,15},{9,10},{10,... | collective-permute-start | bytes 276488 | tf_op jit(solution)/shard_map/ppermute | solution.py:593
  258.1 5.4 %collective-permute-start.61 = (f32[8,320]{1,0:T(8,128)}, f32[8,320]{1,0:T(8,128)S(1)}, u32[]{:S(2)}, u32[]{:S(2)}) collective-permute-start(f32[8,320]{1,0:T(8,128)} %get-tuple-element.148), channel_id=1, source_target_pairs={{0,4},{1,5},{2,6},{3,7},{4,0},{5,1},{6,2},{7,3},{8,12},{9,13},{10,... | collective-permute-start | bytes 30728 | tf_op jit(solution)/shard_map/ppermute | solution.py:593
  259.4 5.0 %collective-permute-start.60 = (f32[8,320]{1,0:T(8,128)}, f32[8,320]{1,0:T(8,128)S(1)}, u32[]{:S(2)}, u32[]{:S(2)}) collective-permute-start(f32[8,320]{1,0:T(8,128)} %get-tuple-element.148), channel_id=1, source_target_pairs={{0,2},{1,7},{2,4},{3,1},{4,6},{5,3},{6,0},{7,5},{8,10},{9,15},{10,... | collective-permute-start | bytes 30728 | tf_op jit(solution)/shard_map/ppermute | solution.py:593
  260.2 5.1 %collective-permute-start.59 = (bf16[128,320]{1,0:T(8,128)(2,1)}, bf16[128,320]{1,0:T(8,128)(2,1)S(1)}, u32[]{:S(2)}, u32[]{:S(2)}) collective-permute-start(bf16[128,320]{1,0:T(8,128)(2,1)} %get-tuple-element.147), channel_id=1, source_target_pairs={{0,1},{1,0},{2,3},{3,2},{4,5},{5,4},{6,7},{7,6},{8,9},{9,8},{10,11... | collective-permute-start | bytes 245768 | tf_op jit(solution)/shard_map/ppermute | solution.py:593
  265.2 1.2 collective-permute-start.62
  275.4 2.7 collective-permute-start.63
  276.1 2.0 collective-permute-start.64
  276.8 9.0 %collective-permute-start.65 = (bf16[8,16,320]{2,1,0:T(8,128)(2,1)}, bf16[8,16,320]{2,1,0:T(8,128)(2,1)S(1)}, u32[]{:S(2)}, u32[]{:S(2)}) collective-permute-start(bf16[8,16,320]{2,1,0:T(8,128)(2,1)} %get-tuple-element.152), channel_id=1, source_target_pairs={{24,16},{25,17},{26,18},{27,19},{28,20},{29,21},{30,22},{31,23}} | collective-permute-start | bytes 245768 | tf_op jit(solution)/shard_map/ppermute | solution.py:589
  (54 other events, 233.7 us)
